TPU v7x, 32 devices: a whole 2x2x4 slice. The times are simulated.
32 devices in a mesh: segment: 4 (over z), seq: 8 (over y, x, core).
Axes of the slice: x: 2, y: 2, z: 4, core: 2. Of those that a mesh axis runs over, the one named last changes fastest.
Arguments:
- sequence: bfloat16 [256, 512, 256], P('seq', 'segment'), may hold values from -6 to 6
- first_factors: bfloat16 [4, 4, 256, 256], P('segment'), may hold values from -0.375 to 0.375
- second_factors: bfloat16 [4, 4, 256, 256], P('segment'), may hold values from -0.375 to 0.375
- kernels: bfloat16 [4, 2, 256, 256], P('segment', None, 'seq'), may hold values from -6 to 6
- gate_scale: float32 [4, 512], P('segment'), may hold values from -2 to 2
- gate_bias: float32 [4, 512], P('segment'), may hold values from -1 to 1
Outputs:
- mixed: bfloat16 [256, 512, 256], P('seq', 'segment')
All inputs are finite; a program needn't handle non-finite values.
Results may differ from a plain program's by a relative error of at most 0.024.
Values may be sent and summed in bfloat16 or wider, within the bound.
A program may use at most 64 MiB of HBM per device.

v0:
```python
import jax
import jax.numpy as jnp
from jax import lax
from jax.sharding import PartitionSpec as P


def transpose_mix(values, first, second):
    rows = values.shape[0]
    width = first.shape[0]
    devices = lax.axis_size("seq")
    mixed = jnp.einsum("pcq,kq->pck", values, first, preferred_element_type=jnp.float32).astype(
        jnp.bfloat16
    )
    folded = second.reshape(width, devices, rows)
    received = lax.all_to_all(mixed, "seq", split_axis=2, concat_axis=2, tiled=True)
    blocks = received.reshape(rows, received.shape[1], devices, rows)
    return jnp.einsum("pcsk,jsp->kcj", blocks, folded, preferred_element_type=jnp.float32)


def layer_apply(values, first, second, kernel_pair, scales, biases):
    kernel_one = kernel_pair[0].astype(jnp.float32)[:, None, :]
    kernel_two = kernel_pair[1].astype(jnp.float32)[:, None, :]
    widened = values.astype(jnp.float32)
    branch_one = (transpose_mix(values, first[0], second[0]) * kernel_one).astype(jnp.bfloat16)
    gating = jax.nn.sigmoid(scales[None, :, None] * widened + biases[None, :, None])
    gated = (transpose_mix(branch_one, first[1], second[1]) * gating).astype(jnp.bfloat16)
    branch_two = (transpose_mix(gated, first[2], second[2]) * kernel_two).astype(jnp.bfloat16)
    return (widened + transpose_mix(branch_two, first[3], second[3])).astype(jnp.bfloat16)


def local(sequence, first_factors, second_factors, kernels, gate_scale, gate_bias):
    position = lax.axis_index("segment")
    local_channels = sequence.shape[1]
    all_first, all_second, all_kernels = (
        lax.all_gather(first_factors, "segment", axis=0, tiled=True),
        lax.all_gather(second_factors, "segment", axis=0, tiled=True),
        lax.all_gather(kernels, "segment", axis=0, tiled=True),
    )
    all_scales, all_biases = (
        lax.all_gather(gate_scale, "segment", axis=0, tiled=True),
        lax.all_gather(gate_bias, "segment", axis=0, tiled=True),
    )
    offset = position * local_channels

    def one_layer(level, current):
        scales = lax.dynamic_slice_in_dim(all_scales[level], offset, local_channels)
        biases = lax.dynamic_slice_in_dim(all_biases[level], offset, local_channels)
        return layer_apply(
            current, all_first[level], all_second[level], all_kernels[level], scales, biases
        )

    return lax.fori_loop(0, all_first.shape[0], one_layer, sequence)


def solution(mesh):
    placed = (
        P("seq", "segment", None),
        P("segment", None, None, None),
        P("segment", None, None, None),
        P("segment", None, "seq", None),
        P("segment", None),
        P("segment", None),
    )
    return jax.shard_map(
        local, mesh=mesh, in_specs=placed, out_specs=P("seq", "segment", None), check_vma=False
    )
```

profile of v0, /device:TPU:25, one launch (start us, length us, event | category | flops | bytes accessed | tf_op | source)
XLA Modules:
  0.0 746.8 jit_solution(15281167645744695565)
XLA Ops:
  11.3 8.5 %all-gather.1 = f32[4,1,512]{2,1,0:T(1,128)S(1)} all-gather(f32[1,1,512]{2,1,0:T(1,128)S(1)} %bitcast.179), channel_id=1, replica_groups=mesh['segment'=4,'seq'=8] {'segment'}, dimensions={0}, use_global_device_ids=true | all-gather | bytes 10240 | tf_op jit(solution)/shard_map/all_gather | solution.py:41
  19.8 9.6 %all-gather = f32[4,1,512]{2,1,0:T(1,128)S(1)} all-gather(f32[1,1,512]{2,1,0:T(1,128)S(1)} %bitcast.180), channel_id=1, replica_groups=mesh['segment'=4,'seq'=8] {'segment'}, dimensions={0}, use_global_device_ids=true | all-gather | bytes 10240 | tf_op jit(solution)/shard_map/all_gather | solution.py:40
  29.4 12.5 %all_gather.17 = bf16[4,2,32,256]{3,2,1,0:T(8,128)(2,1)S(1)} all-gather(bf16[1,2,32,256]{3,2,1,0:T(8,128)(2,1)S(1)} %copy-done), channel_id=1, replica_groups=mesh['segment'=4,'seq'=8] {'segment'}, dimensions={0}, use_global_device_ids=true | all-gather | bytes 163840 | tf_op jit(solution)/shard_map/all_gather | solution.py:37
  42.0 13.8 %all-gather.5.cloned.1.call-done = bf16[4,4,256,256]{3,2,1,0:T(8,128)(2,1)} async-done(((bf16[1,4,256,256]{3,2,1,0:T(8,128)(2,1)}), bf16[4,4,256,256]{3,2,1,0:T(8,128)(2,1)}) %all-gather.5.cloned.1.call-update) | async-done | bytes 2097168 | tf_op jit(solution)/shard_map/all_gather | solution.py:36
  55.8 46.3 %all-gather.7.cloned.1.call-done = bf16[4,4,256,256]{3,2,1,0:T(8,128)(2,1)} async-done(((bf16[1,4,256,256]{3,2,1,0:T(8,128)(2,1)}), bf16[4,4,256,256]{3,2,1,0:T(8,128)(2,1)}) %all-gather.7.cloned.1.call-update) | async-done | bytes 2097168 | tf_op jit(solution)/shard_map/all_gather | solution.py:35
  102.1 634.9 %while.16 = (s32[]{:T(128)}, bf16[32,128,256]{1,2,0:T(8,128)(2,1)S(1)}, bf16[4,4,256,256]{3,2,1,0:T(8,128)(2,1)}, bf16[4,4,256,256]{3,2,1,0:T(8,128)(2,1)}, bf16...) while((s32[]{:T(128)}, ...), condition=%wide.region_1.0_spmd, body=%wide.region_0.0_spmd.sunk | while | flops 4314906624 | bytes 70423912 | solution.py:52
  106.4 4.8 all-to-all-start
  112.4 21.9 %all-to-all-done = bf16[32,128,256]{1,0,2:T(8,128)(2,1)} async-done(((bf16[32,128,256]{1,0,2:T(8,128)(2,1)}), bf16[32,128,256]{1,0,2:T(8,128)(2,1)}, u32[]{:S(2)}, u32[]{:S(2)}) %all-to-all-start) | async-done | bytes 2097184 | tf_op jit(solution)/shard_map/while/body/eval_jaxpr/all_to_all | solution.py:15
  134.3 4.5 convolution_convert_fusion.6
  138.8 4.6 copy.98
  143.4 7.9 %all-to-all-start.1 = ((bf16[32,128,256]{1,0,2:T(8,128)(2,1)}), bf16[32,128,256]{1,0,2:T(8,128)(2,1)}, u32[]{:S(2)}, u32[]{:S(2)}) async-start(bf16[32,128,256]{1,0,2:T(8,128)(2,1)} %copy.98), calls=%async_computation.1 | async-start | bytes 4194304 | tf_op jit(solution)/shard_map/while/body/eval_jaxpr/all_to_all | solution.py:15
  151.4 22.9 %all-to-all-done.1 = bf16[32,128,256]{1,0,2:T(8,128)(2,1)} async-done(((bf16[32,128,256]{1,0,2:T(8,128)(2,1)}), bf16[32,128,256]{1,0,2:T(8,128)(2,1)}, u32[]{:S(2)}, u32[]{:S(2)}) %all-to-all-start.1) | async-done | bytes 2097184 | tf_op jit(solution)/shard_map/while/body/eval_jaxpr/all_to_all | solution.py:15
  174.4 4.8 convolution_convert_fusion.7
  179.2 4.6 copy.99
  183.8 7.9 %all-to-all-start.2 = ((bf16[32,128,256]{1,0,2:T(8,128)(2,1)}), bf16[32,128,256]{1,0,2:T(8,128)(2,1)}, u32[]{:S(2)}, u32[]{:S(2)}) async-start(bf16[32,128,256]{1,0,2:T(8,128)(2,1)} %copy.99), calls=%async_computation.2 | async-start | bytes 4194304 | tf_op jit(solution)/shard_map/while/body/eval_jaxpr/all_to_all | solution.py:15
  191.8 23.0 %all-to-all-done.2 = bf16[32,128,256]{1,0,2:T(8,128)(2,1)} async-done(((bf16[32,128,256]{1,0,2:T(8,128)(2,1)}), bf16[32,128,256]{1,0,2:T(8,128)(2,1)}, u32[]{:S(2)}, u32[]{:S(2)}) %all-to-all-start.2) | async-done | bytes 2097184 | tf_op jit(solution)/shard_map/while/body/eval_jaxpr/all_to_all | solution.py:15
  214.8 4.5 convolution_convert_fusion.8
  219.3 4.6 copy.100
  223.9 7.9 %all-to-all-start.3 = ((bf16[32,128,256]{1,0,2:T(8,128)(2,1)}), bf16[32,128,256]{1,0,2:T(8,128)(2,1)}, u32[]{:S(2)}, u32[]{:S(2)}) async-start(bf16[32,128,256]{1,0,2:T(8,128)(2,1)} %copy.100), calls=%async_computation.3 | async-start | bytes 4194304 | tf_op jit(solution)/shard_map/while/body/eval_jaxpr/all_to_all | solution.py:15
  231.9 23.0 %all-to-all-done.3 = bf16[32,128,256]{1,0,2:T(8,128)(2,1)} async-done(((bf16[32,128,256]{1,0,2:T(8,128)(2,1)}), bf16[32,128,256]{1,0,2:T(8,128)(2,1)}, u32[]{:S(2)}, u32[]{:S(2)}) %all-to-all-start.3) | async-done | bytes 2097184 | tf_op jit(solution)/shard_map/while/body/eval_jaxpr/all_to_all | solution.py:15
  254.9 3.6 fusion.47
  262.8 7.9 %all-to-all-start = ((bf16[32,128,256]{1,0,2:T(8,128)(2,1)}), bf16[32,128,256]{1,0,2:T(8,128)(2,1)}, u32[]{:S(2)}, u32[]{:S(2)}) async-start(bf16[32,128,256]{1,0,2:T(8,128)(2,1)} %copy.97), calls=%async_computation | async-start | bytes 4194304 | tf_op jit(solution)/shard_map/while/body/eval_jaxpr/all_to_all | solution.py:15
  271.9 21.9 %all-to-all-done = bf16[32,128,256]{1,0,2:T(8,128)(2,1)} async-done(((bf16[32,128,256]{1,0,2:T(8,128)(2,1)}), bf16[32,128,256]{1,0,2:T(8,128)(2,1)}, u32[]{:S(2)}, u32[]{:S(2)}) %all-to-all-start) | async-done | bytes 2097184 | tf_op jit(solution)/shard_map/while/body/eval_jaxpr/all_to_all | solution.py:15
  293.8 4.5 convolution_convert_fusion.6
  298.3 4.6 copy.98
  302.9 7.9 %all-to-all-start.1 = ((bf16[32,128,256]{1,0,2:T(8,128)(2,1)}), bf16[32,128,256]{1,0,2:T(8,128)(2,1)}, u32[]{:S(2)}, u32[]{:S(2)}) async-start(bf16[32,128,256]{1,0,2:T(8,128)(2,1)} %copy.98), calls=%async_computation.1 | async-start | bytes 4194304 | tf_op jit(solution)/shard_map/while/body/eval_jaxpr/all_to_all | solution.py:15
  311.0 22.9 %all-to-all-done.1 = bf16[32,128,256]{1,0,2:T(8,128)(2,1)} async-done(((bf16[32,128,256]{1,0,2:T(8,128)(2,1)}), bf16[32,128,256]{1,0,2:T(8,128)(2,1)}, u32[]{:S(2)}, u32[]{:S(2)}) %all-to-all-start.1) | async-done | bytes 2097184 | tf_op jit(solution)/shard_map/while/body/eval_jaxpr/all_to_all | solution.py:15
  333.9 4.8 convolution_convert_fusion.7
  338.8 4.6 copy.99
  343.4 7.9 %all-to-all-start.2 = ((bf16[32,128,256]{1,0,2:T(8,128)(2,1)}), bf16[32,128,256]{1,0,2:T(8,128)(2,1)}, u32[]{:S(2)}, u32[]{:S(2)}) async-start(bf16[32,128,256]{1,0,2:T(8,128)(2,1)} %copy.99), calls=%async_computation.2 | async-start | bytes 4194304 | tf_op jit(solution)/shard_map/while/body/eval_jaxpr/all_to_all | solution.py:15
  351.3 23.0 %all-to-all-done.2 = bf16[32,128,256]{1,0,2:T(8,128)(2,1)} async-done(((bf16[32,128,256]{1,0,2:T(8,128)(2,1)}), bf16[32,128,256]{1,0,2:T(8,128)(2,1)}, u32[]{:S(2)}, u32[]{:S(2)}) %all-to-all-start.2) | async-done | bytes 2097184 | tf_op jit(solution)/shard_map/while/body/eval_jaxpr/all_to_all | solution.py:15
  374.4 4.5 convolution_convert_fusion.8
  378.8 4.6 copy.100
  383.4 7.9 %all-to-all-start.3 = ((bf16[32,128,256]{1,0,2:T(8,128)(2,1)}), bf16[32,128,256]{1,0,2:T(8,128)(2,1)}, u32[]{:S(2)}, u32[]{:S(2)}) async-start(bf16[32,128,256]{1,0,2:T(8,128)(2,1)} %copy.100), calls=%async_computation.3 | async-start | bytes 4194304 | tf_op jit(solution)/shard_map/while/body/eval_jaxpr/all_to_all | solution.py:15
  391.4 23.0 %all-to-all-done.3 = bf16[32,128,256]{1,0,2:T(8,128)(2,1)} async-done(((bf16[32,128,256]{1,0,2:T(8,128)(2,1)}), bf16[32,128,256]{1,0,2:T(8,128)(2,1)}, u32[]{:S(2)}, u32[]{:S(2)}) %all-to-all-start.3) | async-done | bytes 2097184 | tf_op jit(solution)/shard_map/while/body/eval_jaxpr/all_to_all | solution.py:15
  414.4 3.6 fusion.47
  422.3 7.9 %all-to-all-start = ((bf16[32,128,256]{1,0,2:T(8,128)(2,1)}), bf16[32,128,256]{1,0,2:T(8,128)(2,1)}, u32[]{:S(2)}, u32[]{:S(2)}) async-start(bf16[32,128,256]{1,0,2:T(8,128)(2,1)} %copy.97), calls=%async_computation | async-start | bytes 4194304 | tf_op jit(solution)/shard_map/while/body/eval_jaxpr/all_to_all | solution.py:15
  431.5 21.9 %all-to-all-done = bf16[32,128,256]{1,0,2:T(8,128)(2,1)} async-done(((bf16[32,128,256]{1,0,2:T(8,128)(2,1)}), bf16[32,128,256]{1,0,2:T(8,128)(2,1)}, u32[]{:S(2)}, u32[]{:S(2)}) %all-to-all-start) | async-done | bytes 2097184 | tf_op jit(solution)/shard_map/while/body/eval_jaxpr/all_to_all | solution.py:15
  453.3 4.5 convolution_convert_fusion.6
  457.8 4.6 copy.98
  462.4 7.9 %all-to-all-start.1 = ((bf16[32,128,256]{1,0,2:T(8,128)(2,1)}), bf16[32,128,256]{1,0,2:T(8,128)(2,1)}, u32[]{:S(2)}, u32[]{:S(2)}) async-start(bf16[32,128,256]{1,0,2:T(8,128)(2,1)} %copy.98), calls=%async_computation.1 | async-start | bytes 4194304 | tf_op jit(solution)/shard_map/while/body/eval_jaxpr/all_to_all | solution.py:15
  470.5 22.9 %all-to-all-done.1 = bf16[32,128,256]{1,0,2:T(8,128)(2,1)} async-done(((bf16[32,128,256]{1,0,2:T(8,128)(2,1)}), bf16[32,128,256]{1,0,2:T(8,128)(2,1)}, u32[]{:S(2)}, u32[]{:S(2)}) %all-to-all-start.1) | async-done | bytes 2097184 | tf_op jit(solution)/shard_map/while/body/eval_jaxpr/all_to_all | solution.py:15
  493.4 4.8 convolution_convert_fusion.7
  498.3 4.6 copy.99
  502.9 7.9 %all-to-all-start.2 = ((bf16[32,128,256]{1,0,2:T(8,128)(2,1)}), bf16[32,128,256]{1,0,2:T(8,128)(2,1)}, u32[]{:S(2)}, u32[]{:S(2)}) async-start(bf16[32,128,256]{1,0,2:T(8,128)(2,1)} %copy.99), calls=%async_computation.2 | async-start | bytes 4194304 | tf_op jit(solution)/shard_map/while/body/eval_jaxpr/all_to_all | solution.py:15
  510.8 23.0 %all-to-all-done.2 = bf16[32,128,256]{1,0,2:T(8,128)(2,1)} async-done(((bf16[32,128,256]{1,0,2:T(8,128)(2,1)}), bf16[32,128,256]{1,0,2:T(8,128)(2,1)}, u32[]{:S(2)}, u32[]{:S(2)}) %all-to-all-start.2) | async-done | bytes 2097184 | tf_op jit(solution)/shard_map/while/body/eval_jaxpr/all_to_all | solution.py:15
  533.9 4.5 convolution_convert_fusion.8
  538.4 4.6 copy.100
  543.0 7.9 %all-to-all-start.3 = ((bf16[32,128,256]{1,0,2:T(8,128)(2,1)}), bf16[32,128,256]{1,0,2:T(8,128)(2,1)}, u32[]{:S(2)}, u32[]{:S(2)}) async-start(bf16[32,128,256]{1,0,2:T(8,128)(2,1)} %copy.100), calls=%async_computation.3 | async-start | bytes 4194304 | tf_op jit(solution)/shard_map/while/body/eval_jaxpr/all_to_all | solution.py:15
  550.9 23.0 %all-to-all-done.3 = bf16[32,128,256]{1,0,2:T(8,128)(2,1)} async-done(((bf16[32,128,256]{1,0,2:T(8,128)(2,1)}), bf16[32,128,256]{1,0,2:T(8,128)(2,1)}, u32[]{:S(2)}, u32[]{:S(2)}) %all-to-all-start.3) | async-done | bytes 2097184 | tf_op jit(solution)/shard_map/while/body/eval_jaxpr/all_to_all | solution.py:15
  581.8 7.9 %all-to-all-start = ((bf16[32,128,256]{1,0,2:T(8,128)(2,1)}), bf16[32,128,256]{1,0,2:T(8,128)(2,1)}, u32[]{:S(2)}, u32[]{:S(2)}) async-start(bf16[32,128,256]{1,0,2:T(8,128)(2,1)} %copy.97), calls=%async_computation | async-start | bytes 4194304 | tf_op jit(solution)/shard_map/while/body/eval_jaxpr/all_to_all | solution.py:15
  591.0 21.9 %all-to-all-done = bf16[32,128,256]{1,0,2:T(8,128)(2,1)} async-done(((bf16[32,128,256]{1,0,2:T(8,128)(2,1)}), bf16[32,128,256]{1,0,2:T(8,128)(2,1)}, u32[]{:S(2)}, u32[]{:S(2)}) %all-to-all-start) | async-done | bytes 2097184 | tf_op jit(solution)/shard_map/while/body/eval_jaxpr/all_to_all | solution.py:15
  612.9 4.5 convolution_convert_fusion.6
  617.3 4.6 copy.98
  621.9 7.9 %all-to-all-start.1 = ((bf16[32,128,256]{1,0,2:T(8,128)(2,1)}), bf16[32,128,256]{1,0,2:T(8,128)(2,1)}, u32[]{:S(2)}, u32[]{:S(2)}) async-start(bf16[32,128,256]{1,0,2:T(8,128)(2,1)} %copy.98), calls=%async_computation.1 | async-start | bytes 4194304 | tf_op jit(solution)/shard_map/while/body/eval_jaxpr/all_to_all | solution.py:15
  630.0 22.9 %all-to-all-done.1 = bf16[32,128,256]{1,0,2:T(8,128)(2,1)} async-done(((bf16[32,128,256]{1,0,2:T(8,128)(2,1)}), bf16[32,128,256]{1,0,2:T(8,128)(2,1)}, u32[]{:S(2)}, u32[]{:S(2)}) %all-to-all-start.1) | async-done | bytes 2097184 | tf_op jit(solution)/shard_map/while/body/eval_jaxpr/all_to_all | solution.py:15
  652.9 4.8 convolution_convert_fusion.7
  657.8 4.6 copy.99
  662.4 7.9 %all-to-all-start.2 = ((bf16[32,128,256]{1,0,2:T(8,128)(2,1)}), bf16[32,128,256]{1,0,2:T(8,128)(2,1)}, u32[]{:S(2)}, u32[]{:S(2)}) async-start(bf16[32,128,256]{1,0,2:T(8,128)(2,1)} %copy.99), calls=%async_computation.2 | async-start | bytes 4194304 | tf_op jit(solution)/shard_map/while/body/eval_jaxpr/all_to_all | solution.py:15
  670.3 23.0 %all-to-all-done.2 = bf16[32,128,256]{1,0,2:T(8,128)(2,1)} async-done(((bf16[32,128,256]{1,0,2:T(8,128)(2,1)}), bf16[32,128,256]{1,0,2:T(8,128)(2,1)}, u32[]{:S(2)}, u32[]{:S(2)}) %all-to-all-start.2) | async-done | bytes 2097184 | tf_op jit(solution)/shard_map/while/body/eval_jaxpr/all_to_all | solution.py:15
  693.4 4.5 convolution_convert_fusion.8
  697.9 4.6 copy.100
  702.5 7.9 %all-to-all-start.3 = ((bf16[32,128,256]{1,0,2:T(8,128)(2,1)}), bf16[32,128,256]{1,0,2:T(8,128)(2,1)}, u32[]{:S(2)}, u32[]{:S(2)}) async-start(bf16[32,128,256]{1,0,2:T(8,128)(2,1)} %copy.100), calls=%async_computation.3 | async-start | bytes 4194304 | tf_op jit(solution)/shard_map/while/body/eval_jaxpr/all_to_all | solution.py:15
  710.4 23.0 %all-to-all-done.3 = bf16[32,128,256]{1,0,2:T(8,128)(2,1)} async-done(((bf16[32,128,256]{1,0,2:T(8,128)(2,1)}), bf16[32,128,256]{1,0,2:T(8,128)(2,1)}, u32[]{:S(2)}, u32[]{:S(2)}) %all-to-all-start.3) | async-done | bytes 2097184 | tf_op jit(solution)/shard_map/while/body/eval_jaxpr/all_to_all | solution.py:15
  (52 shorter events, 38.3 us)
Async XLA Ops:
  6.5 49.2 %all-gather.5.cloned.1.call-start = ((), (), s32[]{:S(2)}) async-start(), calls=%async_computation.4 | async-start | bytes 2621440 | tf_op jit(solution)/shard_map/all_gather | solution.py:36
  7.3 94.9 %all-gather.7.cloned.1.call-start = ((), (), s32[]{:S(2)}) async-start(), calls=%async_computation.5 | async-start | bytes 2621440 | tf_op jit(solution)/shard_map/all_gather | solution.py:35
  8.0 3.3 copy-start.1
  8.0 11.8 %copy-start.2 = (f32[1,512]{1,0:T(1,128)S(1)}, f32[1,512]{1,0:T(1,128)}, u32[]{:S(2)}) copy-start(f32[1,512]{1,0:T(1,128)} %param.12) | copy-start | bytes 6148
  8.0 21.4 %copy-start = (bf16[1,2,32,256]{3,2,1,0:T(8,128)(2,1)S(1)}, bf16[1,2,32,256]{3,2,1,0:T(8,128)(2,1)}, u32[]{:S(2)}) copy-start(bf16[1,2,32,256]{3,2,1,0:T(8,128)(2,1)} %param.11) | copy-start | bytes 98308
  106.4 27.9 %all-to-all-start = ((bf16[32,128,256]{1,0,2:T(8,128)(2,1)}), bf16[32,128,256]{1,0,2:T(8,128)(2,1)}, u32[]{:S(2)}, u32[]{:S(2)}) async-start(bf16[32,128,256]{1,0,2:T(8,128)(2,1)} %copy.97), calls=%async_computation | async-start | bytes 4194304 | tf_op jit(solution)/shard_map/while/body/eval_jaxpr/all_to_all | solution.py:15
  143.4 31.0 %all-to-all-start.1 = ((bf16[32,128,256]{1,0,2:T(8,128)(2,1)}), bf16[32,128,256]{1,0,2:T(8,128)(2,1)}, u32[]{:S(2)}, u32[]{:S(2)}) async-start(bf16[32,128,256]{1,0,2:T(8,128)(2,1)} %copy.98), calls=%async_computation.1 | async-start | bytes 4194304 | tf_op jit(solution)/shard_map/while/body/eval_jaxpr/all_to_all | solution.py:15
  183.8 31.0 %all-to-all-start.2 = ((bf16[32,128,256]{1,0,2:T(8,128)(2,1)}), bf16[32,128,256]{1,0,2:T(8,128)(2,1)}, u32[]{:S(2)}, u32[]{:S(2)}) async-start(bf16[32,128,256]{1,0,2:T(8,128)(2,1)} %copy.99), calls=%async_computation.2 | async-start | bytes 4194304 | tf_op jit(solution)/shard_map/while/body/eval_jaxpr/all_to_all | solution.py:15
  223.9 31.0 %all-to-all-start.3 = ((bf16[32,128,256]{1,0,2:T(8,128)(2,1)}), bf16[32,128,256]{1,0,2:T(8,128)(2,1)}, u32[]{:S(2)}, u32[]{:S(2)}) async-start(bf16[32,128,256]{1,0,2:T(8,128)(2,1)} %copy.100), calls=%async_computation.3 | async-start | bytes 4194304 | tf_op jit(solution)/shard_map/while/body/eval_jaxpr/all_to_all | solution.py:15
  262.8 31.0 %all-to-all-start = ((bf16[32,128,256]{1,0,2:T(8,128)(2,1)}), bf16[32,128,256]{1,0,2:T(8,128)(2,1)}, u32[]{:S(2)}, u32[]{:S(2)}) async-start(bf16[32,128,256]{1,0,2:T(8,128)(2,1)} %copy.97), calls=%async_computation | async-start | bytes 4194304 | tf_op jit(solution)/shard_map/while/body/eval_jaxpr/all_to_all | solution.py:15
  302.9 31.0 %all-to-all-start.1 = ((bf16[32,128,256]{1,0,2:T(8,128)(2,1)}), bf16[32,128,256]{1,0,2:T(8,128)(2,1)}, u32[]{:S(2)}, u32[]{:S(2)}) async-start(bf16[32,128,256]{1,0,2:T(8,128)(2,1)} %copy.98), calls=%async_computation.1 | async-start | bytes 4194304 | tf_op jit(solution)/shard_map/while/body/eval_jaxpr/all_to_all | solution.py:15
  343.4 31.0 %all-to-all-start.2 = ((bf16[32,128,256]{1,0,2:T(8,128)(2,1)}), bf16[32,128,256]{1,0,2:T(8,128)(2,1)}, u32[]{:S(2)}, u32[]{:S(2)}) async-start(bf16[32,128,256]{1,0,2:T(8,128)(2,1)} %copy.99), calls=%async_computation.2 | async-start | bytes 4194304 | tf_op jit(solution)/shard_map/while/body/eval_jaxpr/all_to_all | solution.py:15
  383.4 31.0 %all-to-all-start.3 = ((bf16[32,128,256]{1,0,2:T(8,128)(2,1)}), bf16[32,128,256]{1,0,2:T(8,128)(2,1)}, u32[]{:S(2)}, u32[]{:S(2)}) async-start(bf16[32,128,256]{1,0,2:T(8,128)(2,1)} %copy.100), calls=%async_computation.3 | async-start | bytes 4194304 | tf_op jit(solution)/shard_map/while/body/eval_jaxpr/all_to_all | solution.py:15
  422.3 31.0 %all-to-all-start = ((bf16[32,128,256]{1,0,2:T(8,128)(2,1)}), bf16[32,128,256]{1,0,2:T(8,128)(2,1)}, u32[]{:S(2)}, u32[]{:S(2)}) async-start(bf16[32,128,256]{1,0,2:T(8,128)(2,1)} %copy.97), calls=%async_computation | async-start | bytes 4194304 | tf_op jit(solution)/shard_map/while/body/eval_jaxpr/all_to_all | solution.py:15
  462.4 31.0 %all-to-all-start.1 = ((bf16[32,128,256]{1,0,2:T(8,128)(2,1)}), bf16[32,128,256]{1,0,2:T(8,128)(2,1)}, u32[]{:S(2)}, u32[]{:S(2)}) async-start(bf16[32,128,256]{1,0,2:T(8,128)(2,1)} %copy.98), calls=%async_computation.1 | async-start | bytes 4194304 | tf_op jit(solution)/shard_map/while/body/eval_jaxpr/all_to_all | solution.py:15
  502.9 31.0 %all-to-all-start.2 = ((bf16[32,128,256]{1,0,2:T(8,128)(2,1)}), bf16[32,128,256]{1,0,2:T(8,128)(2,1)}, u32[]{:S(2)}, u32[]{:S(2)}) async-start(bf16[32,128,256]{1,0,2:T(8,128)(2,1)} %copy.99), calls=%async_computation.2 | async-start | bytes 4194304 | tf_op jit(solution)/shard_map/while/body/eval_jaxpr/all_to_all | solution.py:15
  543.0 31.0 %all-to-all-start.3 = ((bf16[32,128,256]{1,0,2:T(8,128)(2,1)}), bf16[32,128,256]{1,0,2:T(8,128)(2,1)}, u32[]{:S(2)}, u32[]{:S(2)}) async-start(bf16[32,128,256]{1,0,2:T(8,128)(2,1)} %copy.100), calls=%async_computation.3 | async-start | bytes 4194304 | tf_op jit(solution)/shard_map/while/body/eval_jaxpr/all_to_all | solution.py:15
  581.8 31.0 %all-to-all-start = ((bf16[32,128,256]{1,0,2:T(8,128)(2,1)}), bf16[32,128,256]{1,0,2:T(8,128)(2,1)}, u32[]{:S(2)}, u32[]{:S(2)}) async-start(bf16[32,128,256]{1,0,2:T(8,128)(2,1)} %copy.97), calls=%async_computation | async-start | bytes 4194304 | tf_op jit(solution)/shard_map/while/body/eval_jaxpr/all_to_all | solution.py:15
  621.9 31.0 %all-to-all-start.1 = ((bf16[32,128,256]{1,0,2:T(8,128)(2,1)}), bf16[32,128,256]{1,0,2:T(8,128)(2,1)}, u32[]{:S(2)}, u32[]{:S(2)}) async-start(bf16[32,128,256]{1,0,2:T(8,128)(2,1)} %copy.98), calls=%async_computation.1 | async-start | bytes 4194304 | tf_op jit(solution)/shard_map/while/body/eval_jaxpr/all_to_all | solution.py:15
  662.4 31.0 %all-to-all-start.2 = ((bf16[32,128,256]{1,0,2:T(8,128)(2,1)}), bf16[32,128,256]{1,0,2:T(8,128)(2,1)}, u32[]{:S(2)}, u32[]{:S(2)}) async-start(bf16[32,128,256]{1,0,2:T(8,128)(2,1)} %copy.99), calls=%async_computation.2 | async-start | bytes 4194304 | tf_op jit(solution)/shard_map/while/body/eval_jaxpr/all_to_all | solution.py:15
  702.5 31.0 %all-to-all-start.3 = ((bf16[32,128,256]{1,0,2:T(8,128)(2,1)}), bf16[32,128,256]{1,0,2:T(8,128)(2,1)}, u32[]{:S(2)}, u32[]{:S(2)}) async-start(bf16[32,128,256]{1,0,2:T(8,128)(2,1)} %copy.100), calls=%async_computation.3 | async-start | bytes 4194304 | tf_op jit(solution)/shard_map/while/body/eval_jaxpr/all_to_all | solution.py:15
Sparse Core Ops, SparseCore 0:
  8.9 46.8 all-gather.4
  57.3 44.7 all-gather.6
where the time goes:
time: 756 us; the launch traced here: 747 us
  waiting for transfers between devices  425 us (56%)
  starting transfers between devices  123 us (16%)
  local copies, waits for them, and re-layouts  78.4 us (10%)
  matrix products  75.9 us (10%)
  blocking collectives  30.6 us (4%)
  between operations  13.5 us (2%)
    all_to_all x16, waiting for transfers between devices, transpose_mix(): lax.all_to_all(mixed, 'seq', split_axis=2, concat_axis=2, tiled=True)  364 us
    all_to_all x16, starting transfers between devices, transpose_mix(): lax.all_to_all(mixed, 'seq', split_axis=2, concat_axis=2, tiled=True)  123 us
    convert_element_type x16, local copies, waits for them, and re-layouts, transpose_mix(): jnp.einsum('pcq,kq->pck', values, first, preferred_element_type=jnp.float32)  65.8 us
    dot_general x16, matrix products, transpose_mix(): jnp.einsum('pcq,kq->pck', values, first, preferred_element_type=jnp.float32)  61.7 us
    all_gather x1, waiting for transfers between devices, local(): lax.all_gather(first_factors, 'segment', axis=0, tiled=True)  46.3 us
  transfers between devices with their start and end apart: 18, of which 18 were waited for; matrix products, arithmetic and copies ran while one was open for 1% of the time, Pallas kernels for 0%

commit v1 on v0

v1 whole, which is shorter than its diff:
```python
import jax
import jax.numpy as jnp
from jax import lax
from jax.sharding import PartitionSpec as P

F32, BF16 = jnp.float32, jnp.bfloat16


def mm(spec, a, b):
    return jnp.einsum(spec, a, b, preferred_element_type=F32)


def layer_apply(u, f, g, k, scales, biases):
    k = k.astype(F32).transpose(0, 2, 1)
    y = mm("cpq,kq->cpk", u, f[0]).astype(BF16)
    h = (mm("jp,cpk->cjk", g[0], y) * k[0]).astype(BF16)
    y = mm("kq,cqp->ckp", f[1], h).astype(BF16)
    wide = u.astype(F32)
    gate = jax.nn.sigmoid(scales[:, None, None] * wide + biases[:, None, None])
    z = (mm("ckp,jp->ckj", y, g[1]) * gate).astype(BF16)
    y = mm("cpq,kq->cpk", z, f[2]).astype(BF16)
    h = (mm("jp,cpk->cjk", g[2], y) * k[1]).astype(BF16)
    y = mm("kq,cqp->ckp", f[3], h).astype(BF16)
    return (wide + mm("ckp,jp->ckj", y, g[3])).astype(BF16)


def local(sequence, first, second, kernels, scale, bias):
    n = lax.axis_size("seq")
    channels = sequence.shape[1] // n
    gather = lambda a: lax.all_gather(a, "segment", axis=0, tiled=True)
    first, second, scale, bias = gather(first), gather(second), gather(scale), gather(bias)
    kernels = lax.all_gather(gather(kernels), "seq", axis=2, tiled=True)
    u = lax.all_to_all(sequence, "seq", split_axis=1, concat_axis=0, tiled=True)
    u = u.transpose(1, 0, 2)
    offset = (lax.axis_index("segment") * n + lax.axis_index("seq")) * channels
    scale = lax.dynamic_slice_in_dim(scale, offset, channels, 1)
    bias = lax.dynamic_slice_in_dim(bias, offset, channels, 1)
    for l in range(first.shape[0]):
        u = layer_apply(u, first[l], second[l], kernels[l], scale[l], bias[l])
    return lax.all_to_all(u.transpose(1, 0, 2), "seq", split_axis=0, concat_axis=1, tiled=True)


def solution(mesh):
    placed = (
        P("seq", "segment", None),
        P("segment", None, None, None),
        P("segment", None, None, None),
        P("segment", None, "seq", None),
        P("segment", None),
        P("segment", None),
    )
    return jax.shard_map(
        local, mesh=mesh, in_specs=placed, out_specs=P("seq", "segment", None), check_vma=False
    )
```

time: 756 us -> 282 us (0.37)
  waiting for transfers between devices: 425 us -> 96.2 us
  starting transfers between devices: 123 us -> 7.56 us
  local copies, waits for them, and re-layouts: 78.4 us -> 12.8 us
  blocking collectives: 30.6 us -> 58.2 us
  matrix products: 75.9 us -> 87.9 us
    all_to_all x16 -> x1, waiting for transfers between devices: 364 us -> 8.24 us  [local(): u = lax.all_to_all(sequence, 'seq', split_axis=1, concat_axis=0, tiled=True)]
    all_to_all x16 -> x1, starting transfers between devices: 123 us -> 7.48 us  [local(): u = lax.all_to_all(sequence, 'seq', split_axis=1, concat_axis=0, tiled=True)]
    convert_element_type x16 -> x1, local copies, waits for them, and re-layouts: 65.8 us -> 2.76 us  [layer_apply(): return (wide + mm('ckp,jp->ckj', y, g[3])).astype(BF16)]
    all_to_all x0 -> x1, blocking collectives: none -> 29.1 us  [local(): lax.all_to_all(u.transpose(1, 0, 2), 'seq', split_axis=0, concat_axis=1,...]
    all_gather x2 -> x3, waiting for transfers between devices: 60.2 us -> 86.6 us  [the longest x2 86.5 us: local(): gather = lambda a: lax.all_gather(a, 'segment', axis=0, tiled=True)]
    dot_general x20 -> x16, matrix products: 75.9 us -> 87.9 us  [mm(): return jnp.einsum(spec, a, b, preferred_element_type=F32)]
    while x18 -> x0, local copies, waits for them, and re-layouts: 7.69 us -> none  [the longest x2 6.13 us: local(): return lax.fori_loop(0, all_first.shape[0], one_layer, sequence)]
  transfers between devices with their start and end apart: 18 -> 4, of which waited for: 18 -> 3; matrix products, arithmetic and copies ran while one was open for 1% -> 3% of each run, Pallas kernels for 0% -> 0%
where the time goes in v1:
time: 282 us; the launch traced here: 277 us
  waiting for transfers between devices  96.2 us (34%)
  matrix products  87.9 us (31%)
  blocking collectives  58.2 us (21%)
  between operations  13.2 us (5%)
  local copies, waits for them, and re-layouts  12.8 us (5%)
  starting transfers between devices  7.56 us (3%)
    dot_general x16, matrix products, mm(): return jnp.einsum(spec, a, b, preferred_element_type=F32)  87.9 us
    all_gather x2, waiting for transfers between devices, local(): gather = lambda a: lax.all_gather(a, 'segment', axis=0, tiled=True)  86.5 us
    all_gather x3, blocking collectives, local(): gather = lambda a: lax.all_gather(a, 'segment', axis=0, tiled=True)  29.1 us
    all_to_all x1, blocking collectives, local(): lax.all_to_all(u.transpose(1, 0, 2), 'seq', split_axis=0, concat_axis=1,...  29.1 us
    all_to_all x1, waiting for transfers between devices, local(): u = lax.all_to_all(sequence, 'seq', split_axis=1, concat_axis=0, tiled=True)  8.24 us
    all_to_all x1, starting transfers between devices, local(): u = lax.all_to_all(sequence, 'seq', split_axis=1, concat_axis=0, tiled=True)  7.48 us
  transfers between devices with their start and end apart: 4, of which 3 were waited for; matrix products, arithmetic and copies ran while one was open for 3% of the time, Pallas kernels for 0%

profile of v1, /device:TPU:25, one launch (start us, length us, event | category | flops | bytes accessed | tf_op | source)
XLA Modules:
  0.0 277.2 jit_solution(13902113096559762967)
XLA Ops:
  6.5 0.0 all-gather.10.cloned.1.call-start
  6.5 11.5 %all_gather.20 = bf16[4,2,32,256]{3,2,1,0:T(8,128)(2,1)} all-gather(bf16[1,2,32,256]{3,2,1,0:T(8,128)(2,1)} %param.9), channel_id=1, replica_groups=mesh['segment'=4,'seq'=8] {'segment'}, dimensions={0}, use_global_device_ids=true | all-gather | bytes 163840 | tf_op jit(solution)/shard_map/all_gather | solution.py:30
  18.0 0.0 all-gather.10.cloned.1.call-update
  18.0 0.0 all-gather.6.cloned.1.call-start
  18.1 0.7 all-gather.6.cloned.1.call-update
  18.8 0.0 all-gather.8.cloned.1.call-start
  18.8 0.7 all-gather.8.cloned.1.call-update
  19.5 4.1 %copy.9 = bf16[32,128,256]{2,0,1:T(8,128)(2,1)} copy(bf16[32,128,256]{2,1,0:T(8,128)(2,1)} %param.6) | data formatting | bytes 4194304 | tf_op args[0]
  23.6 0.0 copy-start.4
  23.6 0.0 copy-start.5
  23.6 7.5 %all-to-all-start = ((bf16[32,128,256]{2,0,1:T(8,128)(2,1)}), bf16[32,128,256]{2,0,1:T(8,128)(2,1)S(1)}, u32[]{:S(2)}, u32[]{:S(2)}) async-start(bf16[32,128,256]{2,0,1:T(8,128)(2,1)} %copy.9), calls=%async_computation | async-start | bytes 4194304 | tf_op jit(solution)/shard_map/all_to_all | solution.py:33
  31.1 0.0 copy-done.4
  31.1 8.6 %all-gather = f32[4,1,512]{2,1,0:T(1,128)S(1)} all-gather(f32[1,1,512]{2,1,0:T(1,128)S(1)} %bitcast.365), channel_id=1, replica_groups=mesh['segment'=4,'seq'=8] {'segment'}, dimensions={0}, use_global_device_ids=true | all-gather | bytes 10240 | tf_op jit(solution)/shard_map/all_gather | solution.py:30
  39.7 0.0 copy-done.5
  39.7 9.0 %all-gather.1 = f32[4,1,512]{2,1,0:T(1,128)S(1)} all-gather(f32[1,1,512]{2,1,0:T(1,128)S(1)} %bitcast.366), channel_id=1, replica_groups=mesh['segment'=4,'seq'=8] {'segment'}, dimensions={0}, use_global_device_ids=true | all-gather | bytes 10240 | tf_op jit(solution)/shard_map/all_gather | solution.py:30
  48.8 0.1 fusion.95
  48.8 0.1 fusion.96
  48.9 8.2 %all-to-all-done = bf16[32,128,256]{2,0,1:T(8,128)(2,1)S(1)} async-done(((bf16[32,128,256]{2,0,1:T(8,128)(2,1)}), bf16[32,128,256]{2,0,1:T(8,128)(2,1)S(1)}, u32[]{:S(2)}, u32[]{:S(2)}) %all-to-all-start) | async-done | bytes 2097184 | tf_op jit(solution)/shard_map/all_to_all | solution.py:33
  57.2 0.0 copy-start
  57.2 1.3 copy-done
  58.5 1.8 copy.10
  60.3 0.0 all-gather.10.cloned.1.call-done
  60.3 1.4 convert_bitcast_fusion
  61.8 0.9 slice_bitcast_fusion.1
  62.7 40.5 %all-gather.6.cloned.1.call-done = bf16[4,4,256,256]{3,2,1,0:T(8,128)(2,1)} async-done(((bf16[1,4,256,256]{3,2,1,0:T(8,128)(2,1)}), bf16[4,4,256,256]{3,2,1,0:T(8,128)(2,1)}) %all-gather.6.cloned.1.call-update) | async-done | bytes 2097168 | tf_op jit(solution)/shard_map/all_gather | solution.py:30
  103.2 46.1 %all-gather.8.cloned.1.call-done = bf16[4,4,256,256]{3,2,1,0:T(8,128)(2,1)} async-done(((bf16[1,4,256,256]{3,2,1,0:T(8,128)(2,1)}), bf16[4,4,256,256]{3,2,1,0:T(8,128)(2,1)}) %all-gather.8.cloned.1.call-update) | async-done | bytes 2097168 | tf_op jit(solution)/shard_map/all_gather | solution.py:30
  149.3 3.8 %fusion.32 = bf16[16,256,256]{1,2,0:T(8,128)(2,1)} fusion(f32[256,256]{0,1:T(8,128)S(1)} %get-tuple-element.15, bf16[16,256,256]{2,1,0:T(8,128)(2,1)S(1)} %bitcast.360, bf16[4,4,256,256]{3,2,1,0:T(8,128)(2,1)} %all-gather.8.cloned.1.call-done, bf16[4,4,256,256]{3,2,1,0:T(8,128)(2,1)} %all-gather.6.cloned.1.call-done), kind=kOutput, calls=%fused_computation.50 | convolution fusion | flops 1076887552 | bytes 4718592 | tf_op jit(solution)/shard_map/jp,cpk->cjk/dot_general | solution.py:10
  153.1 5.6 %fusion.35 = bf16[16,256,256]{2,1,0:T(8,128)(2,1)} fusion(bf16[16,256,256]{2,1,0:T(8,128)(2,1)S(1)} %bitcast.361, f32[16]{0:T(128)S(1)} %get-tuple-element.24, f32[16]{0:T(128)S(1)} %get-tuple-element.20, bf16[16,256,256]{1,2,0:T(8,128)(2,1)} %fusion.32, bf16[4,4,256,256]{3,2,1,0:T(8,128)(2,1)} %all-gather.8.cloned.1.call-done, ...), kind=kOutput, calls=%fused_computation.54 | convolution fusion | flops 1083179008 | bytes 6553728 | tf_op jit(solution)/shard_map/ckp,jp->ckj/dot_general | solution.py:10
  158.7 4.5 %fusion.31 = bf16[16,256,256]{1,2,0:T(8,128)(2,1)} fusion(f32[256,256]{0,1:T(8,128)S(1)} %get-tuple-element.16, bf16[16,256,256]{2,1,0:T(8,128)(2,1)} %fusion.35, bf16[4,4,256,256]{3,2,1,0:T(8,128)(2,1)} %all-gather.8.cloned.1.call-done, bf16[4,4,256,256]{3,2,1,0:T(8,128)(2,1)} %all-gather.6.cloned.1.call-done), kind=kOutput, calls=%fused_computation.48 | convolution fusion | flops 1076887552 | bytes 4718592 | tf_op jit(solution)/shard_map/jp,cpk->cjk/dot_general | solution.py:10
  163.2 5.7 %fusion.6 = (bf16[16,256,256]{2,1,0:T(8,128)(2,1)}, f32[16,256,256]{2,1,0:T(8,128)}) fusion(bf16[32,8,16,256]{3,0,1,2:T(8,128)(2,1)S(1)} %copy.10, bf16[4,4,256,256]{3,2,1,0:T(8,128)(2,1)} %all-gather.8.cloned.1.call-done, bf16[16,256,256]{1,2,0:T(8,128)(2,1)} %fusion.31, bf16[4,4,256,256]{3,2,1,0:T(8,128)(2,1)} %all-gather.6.cloned.1.call-done), kind=kOutput, calls=%fused_computation.12 | convolution fusion | flops 1077936128 | bytes 10747904 | tf_op jit(solution)/shard_map/ckp,jp->ckj/dot_general | solution.py:10
  168.9 4.5 %fusion.29 = bf16[16,256,256]{1,2,0:T(8,128)(2,1)} fusion(f32[256,256]{0,1:T(8,128)S(1)} %get-tuple-element.13, bf16[16,256,256]{2,1,0:T(8,128)(2,1)} %get-tuple-element.25, bf16[4,4,256,256]{3,2,1,0:T(8,128)(2,1)} %all-gather.8.cloned.1.call-done, bf16[4,4,256,256]{3,2,1,0:T(8,128)(2,1)} %all-gather.6.cloned.1.call-done), kind=kOutput, calls=%fused_computation.44 | convolution fusion | flops 1076887552 | bytes 4718592 | tf_op jit(solution)/shard_map/jp,cpk->cjk/dot_general | solution.py:10
  173.4 6.3 %fusion.34 = bf16[16,256,256]{2,1,0:T(8,128)(2,1)} fusion(bf16[16,256,256]{2,1,0:T(8,128)(2,1)} %get-tuple-element.25, f32[16]{0:T(128)S(1)} %get-tuple-element.23, f32[16]{0:T(128)S(1)} %get-tuple-element.19, bf16[16,256,256]{1,2,0:T(8,128)(2,1)} %fusion.29, bf16[4,4,256,256]{3,2,1,0:T(8,128)(2,1)} %all-gather.8.cloned.1.call-done, ...), kind=kOutput, calls=%fused_computation.53 | convolution fusion | flops 1083179008 | bytes 6553728 | tf_op jit(solution)/shard_map/ckp,jp->ckj/dot_general | solution.py:10
  179.6 4.7 %fusion.28 = bf16[16,256,256]{1,2,0:T(8,128)(2,1)} fusion(f32[256,256]{0,1:T(8,128)S(1)} %get-tuple-element.14, bf16[16,256,256]{2,1,0:T(8,128)(2,1)} %fusion.34, bf16[4,4,256,256]{3,2,1,0:T(8,128)(2,1)} %all-gather.8.cloned.1.call-done, bf16[4,4,256,256]{3,2,1,0:T(8,128)(2,1)} %all-gather.6.cloned.1.call-done), kind=kOutput, calls=%fused_computation.42 | convolution fusion | flops 1076887552 | bytes 4718592 | tf_op jit(solution)/shard_map/jp,cpk->cjk/dot_general | solution.py:10
  184.3 0.0 copy-start.3
  184.3 6.3 %fusion.13 = (bf16[16,256,256]{2,1,0:T(8,128)(2,1)}, f32[16,256,256]{2,1,0:T(8,128)}) fusion(bf16[16,256,256]{2,1,0:T(8,128)(2,1)} %get-tuple-element.25, bf16[4,4,256,256]{3,2,1,0:T(8,128)(2,1)} %all-gather.8.cloned.1.call-done, bf16[16,256,256]{1,2,0:T(8,128)(2,1)} %fusion.28, bf16[4,4,256,256]{3,2,1,0:T(8,128)(2,1)} %all-gather.6.cloned.1.call-done), kind=kOutput, calls=%fused_computation.19 | convolution fusion | flops 1077936128 | bytes 10747904 | tf_op jit(solution)/shard_map/ckp,jp->ckj/dot_general | solution.py:10
  190.6 0.0 copy-done.3
  190.6 4.5 %fusion.26 = bf16[16,256,256]{1,2,0:T(8,128)(2,1)} fusion(f32[256,256]{0,1:T(8,128)S(1)} %copy-done.3, bf16[16,256,256]{2,1,0:T(8,128)(2,1)} %get-tuple-element.27, bf16[4,4,256,256]{3,2,1,0:T(8,128)(2,1)} %all-gather.8.cloned.1.call-done, bf16[4,4,256,256]{3,2,1,0:T(8,128)(2,1)} %all-gather.6.cloned.1.call-done), kind=kOutput, calls=%fused_computation.38 | convolution fusion | flops 1076887552 | bytes 4718592 | tf_op jit(solution)/shard_map/jp,cpk->cjk/dot_general | solution.py:10
  195.1 0.0 copy-start.2
  195.1 6.4 %fusion.33 = bf16[16,256,256]{2,1,0:T(8,128)(2,1)} fusion(bf16[16,256,256]{2,1,0:T(8,128)(2,1)} %get-tuple-element.27, f32[16]{0:T(128)S(1)} %get-tuple-element.22, f32[16]{0:T(128)S(1)} %get-tuple-element.18, bf16[16,256,256]{1,2,0:T(8,128)(2,1)} %fusion.26, bf16[4,4,256,256]{3,2,1,0:T(8,128)(2,1)} %all-gather.8.cloned.1.call-done, ...), kind=kOutput, calls=%fused_computation.52 | convolution fusion | flops 1083179008 | bytes 6553728 | tf_op jit(solution)/shard_map/ckp,jp->ckj/dot_general | solution.py:10
  201.5 0.0 copy-done.2
  201.5 4.5 %fusion.25 = bf16[16,256,256]{1,2,0:T(8,128)(2,1)} fusion(f32[256,256]{0,1:T(8,128)S(1)} %copy-done.2, bf16[16,256,256]{2,1,0:T(8,128)(2,1)} %fusion.33, bf16[4,4,256,256]{3,2,1,0:T(8,128)(2,1)} %all-gather.8.cloned.1.call-done, bf16[4,4,256,256]{3,2,1,0:T(8,128)(2,1)} %all-gather.6.cloned.1.call-done), kind=kOutput, calls=%fused_computation.36 | convolution fusion | flops 1076887552 | bytes 4718592 | tf_op jit(solution)/shard_map/jp,cpk->cjk/dot_general | solution.py:10
  206.0 4.9 %fusion.38 = f32[16,256,256]{2,1,0:T(8,128)} fusion(bf16[16,256,256]{1,2,0:T(8,128)(2,1)} %fusion.25, bf16[4,4,256,256]{3,2,1,0:T(8,128)(2,1)} %all-gather.8.cloned.1.call-done, bf16[4,4,256,256]{3,2,1,0:T(8,128)(2,1)} %all-gather.6.cloned.1.call-done), kind=kOutput, calls=%fused_computation.57 | convolution fusion | flops 1074790400 | bytes 6553600 | tf_op jit(solution)/shard_map/ckp,jp->ckj/dot_general | solution.py:10
  210.9 5.6 %fusion.23 = bf16[16,256,256]{1,2,0:T(8,128)(2,1)} fusion(f32[256,256]{0,1:T(8,128)S(1)} %get-tuple-element.9, bf16[4,4,256,256]{3,2,1,0:T(8,128)(2,1)} %all-gather.8.cloned.1.call-done, bf16[4,4,256,256]{3,2,1,0:T(8,128)(2,1)} %all-gather.6.cloned.1.call-done, f32[16,256,256]{2,1,0:T(8,128)} %fusion.38, bf16[16,256,256]{2,1,0:T(8,128)(2,1)} %get-tuple-element.27), kind=kOutput, calls=%fused_computation.32 | convolution fusion | flops 1080033280 | bytes 8912896 | tf_op jit(solution)/shard_map/jp,cpk->cjk/dot_general | solution.py:10
  216.6 0.0 copy-start.1
  216.6 7.9 %multiply_convert_fusion = bf16[16,256,256]{2,1,0:T(8,128)(2,1)} fusion(f32[16]{0:T(128)S(1)} %get-tuple-element.21, f32[16]{0:T(128)S(1)} %get-tuple-element.17, bf16[16,256,256]{1,2,0:T(8,128)(2,1)} %fusion.23, bf16[4,4,256,256]{3,2,1,0:T(8,128)(2,1)} %all-gather.8.cloned.1.call-done, bf16[4,4,256,256]{3,2,1,0:T(8,128)(2,1)} %all-gather.6.cloned.1.call-done, ...), kind=kOutput, calls=%fused_computation.51 | convolution fusion | flops 1086324736 | bytes 10748032 | tf_op jit(solution)/shard_map/ckp,jp->ckj/dot_general | solution.py:10
  224.4 0.0 copy-done.1
  224.4 4.5 %fusion.22 = bf16[16,256,256]{1,2,0:T(8,128)(2,1)} fusion(f32[256,256]{0,1:T(8,128)S(1)} %copy-done.1, bf16[16,256,256]{2,1,0:T(8,128)(2,1)} %multiply_convert_fusion, bf16[4,4,256,256]{3,2,1,0:T(8,128)(2,1)} %all-gather.8.cloned.1.call-done, bf16[4,4,256,256]{3,2,1,0:T(8,128)(2,1)} %all-gather.6.cloned.1.call-done), kind=kOutput, calls=%fused_computation.30 | convolution fusion | flops 1076887552 | bytes 4718592 | tf_op jit(solution)/shard_map/jp,cpk->cjk/dot_general | solution.py:10
  228.9 8.3 %fusion.21 = bf16[256,16,256]{2,0,1:T(8,128)(2,1)} fusion(f32[16,256,256]{2,1,0:T(8,128)} %fusion.38, f32[16,256,256]{2,1,0:T(8,128)} %get-tuple-element.28, f32[16,256,256]{2,1,0:T(8,128)} %get-tuple-element.26, bf16[256,16,256]{2,0,1:T(8,128)(2,1)S(1)} %bitcast.362, bf16[16,256,256]{1,2,0:T(8,128)(2,1)} %fusion.22, ...), kind=kOutput, calls=%fused_computation.28 | convolution fusion | flops 1087373312 | bytes 19136512 | tf_op jit(solution)/shard_map/ckp,jp->ckj/dot_general | solution.py:10
  237.2 2.8 copy.11
  240.0 29.1 %all_to_all.36 = bf16[256,16,256]{2,1,0:T(8,128)(2,1)S(1)} all-to-all(bf16[256,16,256]{2,1,0:T(8,128)(2,1)S(1)} %copy.11), channel_id=1, replica_groups=mesh['segment'=4,'seq'=8] {'seq'}, dimensions={0} | all-to-all | bytes 4194304 | tf_op jit(solution)/shard_map/all_to_all | solution.py:40
  269.1 1.6 copy.12
  (2 shorter events, 0.1 us)
Async XLA Ops:
  6.5 53.8 %all-gather.10.cloned.1.call-start = ((), (), s32[]{:S(2)}) async-start(), calls=%async_computation.4 | async-start | bytes 1179648 | tf_op jit(solution)/shard_map/all_gather | solution.py:32
  18.0 85.2 %all-gather.6.cloned.1.call-start = ((), (), s32[]{:S(2)}) async-start(), calls=%async_computation.2 | async-start | bytes 2621440 | tf_op jit(solution)/shard_map/all_gather | solution.py:30
  18.8 130.5 %all-gather.8.cloned.1.call-start = ((), (), s32[]{:S(2)}) async-start(), calls=%async_computation.3 | async-start | bytes 2621440 | tf_op jit(solution)/shard_map/all_gather | solution.py:30
  23.6 7.5 %copy-start.4 = (f32[1,512]{1,0:T(1,128)S(1)}, f32[1,512]{1,0:T(1,128)}, u32[]{:S(2)}) copy-start(f32[1,512]{1,0:T(1,128)} %param.10) | copy-start | bytes 6148
  23.6 16.1 %copy-start.5 = (f32[1,512]{1,0:T(1,128)S(1)}, f32[1,512]{1,0:T(1,128)}, u32[]{:S(2)}) copy-start(f32[1,512]{1,0:T(1,128)} %param.11) | copy-start | bytes 6148
  23.6 33.5 %all-to-all-start = ((bf16[32,128,256]{2,0,1:T(8,128)(2,1)}), bf16[32,128,256]{2,0,1:T(8,128)(2,1)S(1)}, u32[]{:S(2)}, u32[]{:S(2)}) async-start(bf16[32,128,256]{2,0,1:T(8,128)(2,1)} %copy.9), calls=%async_computation | async-start | bytes 4194304 | tf_op jit(solution)/shard_map/all_to_all | solution.py:33
  57.2 1.3 copy-start
  184.3 6.3 %copy-start.3 = (f32[256,256]{0,1:T(8,128)S(1)}, f32[256,256]{0,1:T(8,128)}, u32[]{:S(2)}) copy-start(f32[256,256]{0,1:T(8,128)} %get-tuple-element.30) | copy-start | bytes 786436
  195.1 6.4 %copy-start.2 = (f32[256,256]{0,1:T(8,128)S(1)}, f32[256,256]{0,1:T(8,128)}, u32[]{:S(2)}) copy-start(f32[256,256]{0,1:T(8,128)} %get-tuple-element.29) | copy-start | bytes 786436
  216.6 7.9 %copy-start.1 = (f32[256,256]{0,1:T(8,128)S(1)}, f32[256,256]{0,1:T(8,128)}, u32[]{:S(2)}) copy-start(f32[256,256]{0,1:T(8,128)} %get-tuple-element.10) | copy-start | bytes 786436
Sparse Core Ops, SparseCore 0:
  18.1 36.6 all-gather.9
  56.4 46.7 all-gather.5
  104.8 44.4 all-gather.7

commit v2 on v1

v2 whole, which is shorter than its diff:
```python
import functools

import jax
import jax.numpy as jnp
from jax import lax
from jax.experimental import pallas as pl
from jax.experimental.pallas import tpu as pltpu
from jax.sharding import PartitionSpec as P

F32, BF16 = jnp.float32, jnp.bfloat16
NT = (((1,), (1,)), ((), ()))
NN = (((1,), (0,)), ((), ()))


def dot(a, b, dims):
    return lax.dot_general(a, b, dims, preferred_element_type=F32)


def kernel(
    n, nz, group, x_in, f_own, g_own, k_own, gate_own, out,
    x, w, kk, gates, kt, gv,
    own_sem, in_send, in_recv, out_send, out_recv, out_own,
    up_send, down_send, z_recv, sib_send, sib_recv, k_send, k_recv,
):
    s, z = lax.axis_index("seq"), lax.axis_index("segment")
    core = lax.rem(s, 2)
    sib = s + 1 - 2 * core
    channels, _, rows, radix = x.shape
    groups = channels // group
    maps = w.shape[2]
    pieces = maps + 2

    def peer(d):
        return lax.rem(s + d, n)

    def remote(src, dst, send, recv, **where):
        return pltpu.make_async_remote_copy(
            src_ref=src, dst_ref=dst, send_sem=send, recv_sem=recv,
            device_id=where, device_id_type=pl.DeviceIdType.MESH,
        )

    def in_copy(g, d):
        t = peer(d)
        here = pl.ds(g * group, group)
        return remote(
            x_in.at[t, here], x.at[here, s], in_send.at[g, d], in_recv.at[g, d], seq=t
        )

    def out_copy(g, d):
        t = peer(d)
        here = pl.ds(g * group, group)
        return remote(
            x.at[here, t], out.at[s, here], out_send.at[g, d], out_recv.at[g, d], seq=t
        )

    def z_views(l):
        return [w.at[core, l, r] for r in range(maps)] + [kk.at[l, s], gates.at[l]]

    def z_copies(l, up):
        sem = up_send if up else down_send
        target = z + 1 if up else z - 1
        return [
            remote(v, v, sem.at[l, i], z_recv.at[l, i], segment=target)
            for i, v in enumerate(z_views(l))
        ]

    def sib_copy(l, r):
        v = w.at[core, l, r]
        return remote(v, v, sib_send.at[l, r], sib_recv.at[l, r], seq=sib)

    def sib_wait(l, r):
        v = w.at[1 - core, l, r]
        remote(v, v, sib_send.at[l, r], sib_recv.at[l, r], seq=sib).wait_recv()

    def k_copy(l, d):
        v = kk.at[l, s]
        return remote(v, v, k_send.at[l, d], k_recv.at[l, d], seq=peer(d))

    def k_wait(l, d):
        v = kk.at[l, lax.rem(s + n - d, n)]
        remote(v, v, k_send.at[l, d], k_recv.at[l, d], seq=peer(d)).wait_recv()

    def in_wait(g, d):
        here = pl.ds(g * group, group)
        v = x.at[here, lax.rem(s + n - d, n)]
        remote(v, v, in_send.at[g, d], in_recv.at[g, d], seq=peer(d)).wait_recv()

    def out_wait(g, d):
        here = pl.ds(g * group, group)
        v = out.at[lax.rem(s + n - d, n), here]
        remote(v, v, out_send.at[g, d], out_recv.at[g, d], seq=peer(d)).wait_recv()

    def k_spread(l):
        def one(d, _):
            k_copy(l, d).start()
            return 0

        lax.fori_loop(1, n, one, 0)

    own = [
        pltpu.make_async_copy(f_own.at[0], w.at[0, z], own_sem.at[0]),
        pltpu.make_async_copy(g_own.at[0], w.at[1, z], own_sem.at[1]),
        pltpu.make_async_copy(k_own.at[0], kk.at[z, s], own_sem.at[2]),
        pltpu.make_async_copy(gate_own.at[0], gates.at[z], own_sem.at[3]),
        pltpu.make_async_copy(x_in.at[s], x.at[:, s], own_sem.at[4]),
    ]
    for c in own:
        c.start()

    barrier = pltpu.get_barrier_semaphore()
    mesh_id = pl.DeviceIdType.MESH

    def greet(d, _):
        pl.semaphore_signal(barrier, inc=1, device_id={"seq": peer(d)}, device_id_type=mesh_id)
        return 0

    lax.fori_loop(1, n, greet, 0)

    @pl.when(z > 0)
    def _():
        pl.semaphore_signal(barrier, inc=1, device_id={"segment": z - 1}, device_id_type=mesh_id)

    @pl.when(z < nz - 1)
    def _():
        pl.semaphore_signal(barrier, inc=1, device_id={"segment": z + 1}, device_id_type=mesh_id)

    beside = (z + nz - 1) // nz + (2 * nz - 2 - z) // nz
    pl.semaphore_wait(barrier, n - 1 + beside)

    for c in own[:4]:
        c.wait()

    @pl.when(z == 0)
    def _():
        for c in z_copies(z, True):
            c.start()

    @pl.when(z > 0)
    def _():
        for c in z_copies(z, False):
            c.start()

    def send_in(g, _):
        def one(d, _):
            in_copy(g, d).start()
            return 0

        lax.fori_loop(1, n, one, 0)

        @pl.when(g == 0)
        def _():
            k_spread(z)

        return 0

    lax.fori_loop(0, groups, send_in, 0)
    own[4].wait()

    def relay(l, up):
        arriving = z_copies(l, up)
        for i, c in enumerate(arriving):
            c.wait_recv()

            @pl.when((z < nz - 1) if up else (z > 0))
            def _():
                c.start()

            if i < maps:
                sib_copy(l, i).start()
            elif i == maps:
                k_spread(l)

    def stage(l):
        @pl.when(z > l)
        def _():
            relay(l, True)

        @pl.when(jnp.logical_and(z == l + 1, z < nz - 1))
        def _():
            for c in z_copies(z, True):
                c.start()

        @pl.when(z + l + 1 < nz)
        def _():
            relay(z + l + 1, False)

        @pl.when(z != l)
        def _():
            for r in range(maps):
                sib_wait(l, r)

        def one(d, _):
            k_wait(l, d)
            return 0

        lax.fori_loop(1, n, one, 0)

    def load(c):
        v = x[c]
        if rows % 16:
            v = v.astype(F32)
        return v.reshape(radix, radix).astype(BF16)

    def store(c, v):
        x[c] = v.reshape(n, rows, radix).astype(BF16)

    total = gates.shape[2]
    first_channel = (z * n + s) * channels

    def prepare(l):
        for i in range(2):
            full = kk[l, :, i].astype(F32).reshape(radix, radix)
            kt[i] = full.T
        pick = lax.broadcasted_iota(jnp.int32, (channels, total), 1) == (
            lax.broadcasted_iota(jnp.int32, (channels, total), 0) + first_channel
        )
        both = gates[l]
        for i in range(2):
            col = jnp.sum(jnp.where(pick, both[i : i + 1], 0.0), axis=1, keepdims=True)
            gv[i] = jnp.broadcast_to(0.5 * col, (channels, radix)).reshape(channels, 1, radix)

    def compute(l, g):
        ids = [g * group + i for i in range(group)]
        f = [w[0, l, r] for r in range(maps)]
        h = [w[1, l, r] for r in range(maps)]
        u = [load(c) for c in ids]
        y = [dot(v, f[0], NT).astype(BF16) for v in u]
        y = [(dot(h[0], v, NN) * kt[0]).astype(BF16) for v in y]
        y = [dot(f[1], v, NN).astype(BF16) for v in y]
        gate = [0.5 + 0.5 * jnp.tanh(gv[0, c] * v.astype(F32) + gv[1, c]) for c, v in zip(ids, u)]
        y = [(dot(v, h[1], NT) * q).astype(BF16) for v, q in zip(y, gate)]
        y = [dot(v, f[2], NT).astype(BF16) for v in y]
        y = [(dot(h[2], v, NN) * kt[1]).astype(BF16) for v in y]
        y = [dot(f[3], v, NN).astype(BF16) for v in y]
        for c, v, base in zip(ids, y, u):
            store(c, base.astype(F32) + dot(v, h[3], NT))

    layers = w.shape[1]

    def layer(l, _):
        stage(l)
        prepare(l)

        def one(g, _):
            @pl.when(l == 0)
            def _():
                def arrive(d, _):
                    in_wait(g, d)
                    return 0

                lax.fori_loop(1, n, arrive, 0)

            compute(l, g)

            @pl.when(l == layers - 1)
            def _():
                def leave(d, _):
                    out_copy(g, d).start()
                    return 0

                lax.fori_loop(1, n, leave, 0)
                here = pl.ds(g * group, group)
                pltpu.make_async_copy(x.at[here, s], out.at[s, here], out_own.at[g]).start()

            return 0

        return lax.fori_loop(0, groups, one, 0)

    lax.fori_loop(0, layers, layer, 0)

    def drain_group(g, _):
        def one(d, _):
            in_copy(g, d).wait_send()
            out_copy(g, d).wait_send()
            out_wait(g, d)
            return 0

        lax.fori_loop(1, n, one, 0)
        here = pl.ds(g * group, group)
        pltpu.make_async_copy(x.at[here, s], out.at[s, here], out_own.at[g]).wait()
        return 0

    lax.fori_loop(0, groups, drain_group, 0)

    def drain_layer(l, _):
        def one(d, _):
            k_copy(l, d).wait_send()
            return 0

        lax.fori_loop(1, n, one, 0)

        @pl.when(z != l)
        def _():
            for r in range(maps):
                sib_copy(l, r).wait_send()

        @pl.when(jnp.logical_and(l <= z, z < nz - 1))
        def _():
            for c in z_copies(l, True):
                c.wait_send()

        @pl.when(jnp.logical_and(l >= z, z > 0))
        def _():
            for c in z_copies(l, False):
                c.wait_send()

        return 0

    lax.fori_loop(0, layers, drain_layer, 0)


def solution(mesh):
    n, nz = mesh.shape["seq"], mesh.shape["segment"]

    def local(sequence, first, second, kernels, scale, bias):
        rows, local_channels, radix = sequence.shape
        channels = local_channels // n
        group = min(4, channels)
        groups = channels // group
        maps = first.shape[1]
        layers = nz
        total = scale.shape[1]
        x_in = sequence.transpose(1, 0, 2).reshape(n, channels, rows, radix)
        gate = jnp.stack([scale, bias], axis=1)
        sem = pltpu.SemaphoreType.DMA
        anywhere = pl.BlockSpec(memory_space=pl.ANY)
        result = pl.pallas_call(
            functools.partial(kernel, n, nz, group),
            out_shape=jax.ShapeDtypeStruct((n, channels, rows, radix), BF16),
            in_specs=[anywhere] * 5,
            out_specs=anywhere,
            scratch_shapes=[
                pltpu.VMEM((channels, n, rows, radix), BF16),
                pltpu.VMEM((2, layers, maps, radix, radix), BF16),
                pltpu.VMEM((layers, n, 2, rows, radix), BF16),
                pltpu.VMEM((layers, 2, total), F32),
                pltpu.VMEM((2, radix, radix), F32),
                pltpu.VMEM((2, channels, 1, radix), F32),
                sem((5,)),
                sem((groups, n)),
                sem((groups, n)),
                sem((groups, n)),
                sem((groups, n)),
                sem((groups,)),
                sem((layers, maps + 2)),
                sem((layers, maps + 2)),
                sem((layers, maps + 2)),
                sem((layers, maps)),
                sem((layers, maps)),
                sem((layers, n)),
                sem((layers, n)),
            ],
            compiler_params=pltpu.CompilerParams(
                collective_id=0, has_side_effects=True, vmem_limit_bytes=56 * 2**20
            ),
        )(x_in, first, second, kernels, gate)
        return result.reshape(local_channels, rows, radix).transpose(1, 0, 2)

    placed = (
        P("seq", "segment", None),
        P("segment", None, None, None),
        P("segment", None, None, None),
        P("segment", None, "seq", None),
        P("segment", None),
        P("segment", None),
    )
    return jax.shard_map(
        local, mesh=mesh, in_specs=placed, out_specs=P("seq", "segment", None), check_vma=False
    )
```

time: 282 us -> 117 us (0.41); the launches traced: 277 us -> 117 us
  Pallas kernels: 0 us -> 107 us
  waiting for transfers between devices: 96.2 us -> 0 us
  matrix products: 87.9 us -> 0 us
  blocking collectives: 58.2 us -> 0 us
  between operations: 13.2 us -> 0.01 us
  starting transfers between devices: 7.56 us -> 0 us
  local copies, waits for them, and re-layouts: 12.8 us -> 8.17 us
    pallas_call x0 -> x1, Pallas kernels: none -> 107 us  [local(): pl.pallas_call(functools.partial(kernel, n, nz, group), out_shape=jax.Sha...]
    dot_general x16 -> x0, matrix products: 87.9 us -> none  [mm(): return jnp.einsum(spec, a, b, preferred_element_type=F32)]
    all_gather x3 -> x0, waiting for transfers between devices: 86.6 us -> none  [the longest x2 86.5 us: local(): gather = lambda a: lax.all_gather(a, 'segment', axis=0, tiled=True)]
    all_gather x3 -> x0, blocking collectives: 29.1 us -> none  [local(): gather = lambda a: lax.all_gather(a, 'segment', axis=0, tiled=True)]
    all_to_all x1 -> x0, blocking collectives: 29.1 us -> none  [local(): lax.all_to_all(u.transpose(1, 0, 2), 'seq', split_axis=0, concat_axis=1,...]
    all_to_all x1 -> x0, waiting for transfers between devices: 8.24 us -> none  [local(): u = lax.all_to_all(sequence, 'seq', split_axis=1, concat_axis=0, tiled=True)]
    all_to_all x1 -> x0, starting transfers between devices: 7.48 us -> none  [local(): u = lax.all_to_all(sequence, 'seq', split_axis=1, concat_axis=0, tiled=True)]
    unnamed x13 -> x0, local copies, waits for them, and re-layouts: 5.42 us -> none
  transfers between devices with their start and end apart: 4 -> 0, of which waited for: 3 -> 0; matrix products, arithmetic and copies ran while one was open for 3% -> 0% of each run, Pallas kernels for 0% -> 0%
where the time goes in v2:
time: 117 us
  Pallas kernels  107 us (91%)
  local copies, waits for them, and re-layouts  8.17 us (7%)
  other arithmetic  1.3 us (1%)
    pallas_call x1, Pallas kernels, local(): pl.pallas_call(functools.partial(kernel, n, nz, group), out_shape=jax.Sha...  107 us
    reshape x1, local copies, waits for them, and re-layouts, local(): return result.reshape(local_channels, rows, radix).transpose(1, 0, 2)  4.08 us
    transpose x1, local copies, waits for them, and re-layouts, local(): x_in = sequence.transpose(1, 0, 2).reshape(n, channels, rows, radix)  4.08 us

profile of v2, /device:TPU:25, one launch (start us, length us, event | category | flops | bytes accessed | tf_op | source)
XLA Modules:
  0.0 116.9 jit_solution(4477868123397972401)
XLA Ops:
  0.0 1.3 %pad_maximum_fusion.gate_own = f32[1,2,512]{2,1,0:T(2,128)} fusion(f32[1,1,512]{2,1,0:T(1,128)} %bitcast.11, f32[1,1,512]{2,1,0:T(1,128)} %bitcast.12), kind=kLoop, calls=%fused_computation.1 | loop fusion | flops 1024 | bytes 8192 | tf_op jit(solution)/shard_map/stack | solution.py:324
  1.3 4.1 %copy.7 = bf16[128,32,256]{2,1,0:T(8,128)(2,1)} copy(bf16[128,32,256]{2,0,1:T(8,128)(2,1)} %bitcast.10) | data formatting | bytes 4194304 | tf_op jit(solution)/shard_map/transpose | solution.py:323
  5.4 107.4 %shard_map.64 = bf16[8,16,32,256]{3,2,1,0:T(8,128)(2,1)} custom-call(bf16[8,16,32,256]{3,2,1,0:T(8,128)(2,1)} %bitcast.9, bf16[1,4,256,256]{3,2,1,0:T(8,128)(2,1)} %f_own.1, bf16[1,4,256,256]{3,2,1,0:T(8,128)(2,1)} %g_own.1, bf16[1,2,32,256]{3,2,1,0:T(8,128)(2,1)} %k_own.1, f32[1,2,512]{2,1,0:T(2,128)} %pad_maximum_fusion.gate_own), custom_call_target="tpu_custom_call" | custom-call | tf_op jit(solution)/shard_map/pallas_call | solution.py:327
  112.8 4.1 %copy.10 = bf16[128,32,256]{2,0,1:T(8,128)(2,1)} copy(bf16[128,32,256]{2,1,0:T(8,128)(2,1)} %bitcast.8) | data formatting | bytes 4194304 | tf_op jit(solution)/shard_map/reshape | solution.py:357

commit v3 on v2

v3 whole, which is shorter than its diff:
```python
import functools

import jax
import jax.numpy as jnp
from jax import lax
from jax.experimental import pallas as pl
from jax.experimental.pallas import tpu as pltpu
from jax.sharding import PartitionSpec as P

F32, BF16 = jnp.float32, jnp.bfloat16
NT = (((1,), (1,)), ((), ()))
NN = (((1,), (0,)), ((), ()))


def dot(a, b, dims):
    return lax.dot_general(a, b, dims, preferred_element_type=F32)


def kernel(
    n, nz, group, x_in, f_own, g_own, k_own, gate_own, out,
    x, w, kk, gates, kt, gv,
    own_sem, in_send, in_recv, out_send, out_recv, out_own,
    up_send, down_send, z_recv, sib_send, sib_recv,
    kz_send, kz_recv, gz_send, gz_recv, ks_send, ks_recv, kf_send, kf_recv,
):
    s, z = lax.axis_index("seq"), lax.axis_index("segment")
    core = lax.rem(s, 2)
    sib = s + 1 - 2 * core
    channels, _, rows, radix = x.shape
    groups = channels // group
    maps = w.shape[2]
    layers = w.shape[1]
    half = n // 2

    def peer(d):
        return lax.rem(s + d, n)

    def remote(src, dst, send, recv, **where):
        return pltpu.make_async_remote_copy(
            src_ref=src, dst_ref=dst, send_sem=send, recv_sem=recv,
            device_id=where, device_id_type=pl.DeviceIdType.MESH,
        )

    def in_copy(g, d):
        t = peer(d)
        here = pl.ds(g * group, group)
        return remote(
            x_in.at[t, here], x.at[here, s], in_send.at[g, d], in_recv.at[g, d], seq=t
        )

    def out_copy(g, d):
        t = peer(d)
        here = pl.ds(g * group, group)
        return remote(
            x.at[here, t], out.at[s, here], out_send.at[g, d], out_recv.at[g, d], seq=t
        )

    def z_copy(l, i, up):
        v = w.at[core, l, i]
        sem = up_send if up else down_send
        return remote(v, v, sem.at[l, i], z_recv.at[l, i], segment=z + 1 if up else z - 1)

    def sib_copy(l, r):
        v = w.at[core, l, r]
        return remote(v, v, sib_send.at[l, r], sib_recv.at[l, r], seq=sib)

    def sib_wait(l, r):
        v = w.at[1 - core, l, r]
        remote(v, v, sib_send.at[l, r], sib_recv.at[l, r], seq=sib).wait_recv()

    def kz_copy(d, l):
        to = lax.rem(z + d, nz)
        return (
            remote(kk.at[s, l], kk.at[s, l], kz_send.at[d], kz_recv.at[d], segment=to),
            remote(gates.at[l], gates.at[l], gz_send.at[d], gz_recv.at[d], segment=to),
        )

    def ks_copy(d, owner):
        v = kk.at[owner]
        return remote(v, v, ks_send.at[d], ks_recv.at[d], seq=lax.rem(s + 2 * d, n))

    def kf_copy(d, owner):
        v = kk.at[owner]
        return remote(v, v, kf_send.at[d], kf_recv.at[d], seq=sib)

    def in_wait(g, d):
        here = pl.ds(g * group, group)
        v = x.at[here, lax.rem(s + n - d, n)]
        remote(v, v, in_send.at[g, d], in_recv.at[g, d], seq=peer(d)).wait_recv()

    def out_wait(g, d):
        here = pl.ds(g * group, group)
        v = out.at[lax.rem(s + n - d, n), here]
        remote(v, v, out_send.at[g, d], out_recv.at[g, d], seq=peer(d)).wait_recv()

    own = [
        pltpu.make_async_copy(f_own.at[0], w.at[0, z], own_sem.at[0]),
        pltpu.make_async_copy(g_own.at[0], w.at[1, z], own_sem.at[1]),
        pltpu.make_async_copy(k_own.at[0], kk.at[s, z], own_sem.at[2]),
        pltpu.make_async_copy(gate_own.at[0], gates.at[z], own_sem.at[3]),
        pltpu.make_async_copy(x_in.at[s], x.at[:, s], own_sem.at[4]),
    ]
    for c in own:
        c.start()

    barrier = pltpu.get_barrier_semaphore()
    mesh_id = pl.DeviceIdType.MESH

    def greet(d, _):
        pl.semaphore_signal(barrier, inc=1, device_id={"seq": peer(d)}, device_id_type=mesh_id)
        return 0

    lax.fori_loop(1, n, greet, 0)

    def greet_z(d, _):
        to = lax.rem(z + d, nz)
        pl.semaphore_signal(barrier, inc=1, device_id={"segment": to}, device_id_type=mesh_id)
        return 0

    lax.fori_loop(1, nz, greet_z, 0)
    pl.semaphore_wait(barrier, n + nz - 2)

    for c in own[:4]:
        c.wait()

    for d in range(1, nz):
        for c in kz_copy(d, z):
            c.start()

    def send_in(g, _):
        def one(d, _):
            in_copy(g, d).start()
            return 0

        return lax.fori_loop(1, n, one, 0)

    send_in(0, 0)

    def send_own(up):
        for i in range(maps):
            z_copy(z, i, up).start()

    @pl.when(z == 0)
    def _():
        send_own(True)

    @pl.when(z > 0)
    def _():
        send_own(False)

    for d in range(1, nz):
        for c in kz_copy(d, lax.rem(z + nz - d, nz)):
            c.wait_recv()
    for d in range(1, half):
        ks_copy(d, s).start()
    kf_copy(0, s).start()
    lax.fori_loop(1, groups, send_in, 0)
    own[4].wait()

    def relay(l, i, up):
        c = z_copy(l, i, up)
        c.wait_recv()

        @pl.when((z < nz - 1) if up else (z > 0))
        def _():
            c.start()

        sib_copy(l, i).start()

    def stage(k, i):
        @pl.when(z > k)
        def _():
            relay(k, i, True)

        @pl.when(z + k + 1 < nz)
        def _():
            relay(z + k + 1, i, False)

    def stage_end(k):
        @pl.when(jnp.logical_and(z == k + 1, z < nz - 1))
        def _():
            send_own(True)

    def sib_arrive(l):
        @pl.when(z != l)
        def _():
            for r in range(maps):
                sib_wait(l, r)

    for i in range(maps):
        stage(0, i)
    stage_end(0)

    def load(c):
        v = x[c]
        if rows % 16:
            v = v.astype(F32)
        return v.reshape(radix, radix).astype(BF16)

    def store(c, v):
        x[c] = v.reshape(n, rows, radix).astype(BF16)

    total = gates.shape[2]
    first_channel = (z * n + s) * channels

    def prepare(l, _):
        for i in range(2):
            full = kk[:, l, i].astype(F32).reshape(radix, radix)
            kt[l, i] = full.T
        pick = lax.broadcasted_iota(jnp.int32, (channels, total), 1) == (
            lax.broadcasted_iota(jnp.int32, (channels, total), 0) + first_channel
        )
        both = gates[l]
        for i in range(2):
            col = jnp.sum(jnp.where(pick, both[i : i + 1], 0.0), axis=1, keepdims=True)
            wide = jnp.broadcast_to(0.5 * col, (channels, radix))
            gv[l, i] = wide.reshape(channels, 1, radix)
        return 0

    def compute(l, g):
        ids = [g * group + i for i in range(group)]
        f = [w[0, l, r] for r in range(maps)]
        h = [w[1, l, r] for r in range(maps)]
        u = [load(c) for c in ids]
        y = [dot(v, f[0], NT).astype(BF16) for v in u]
        y = [(dot(h[0], v, NN) * kt[l, 0]).astype(BF16) for v in y]
        y = [dot(f[1], v, NN).astype(BF16) for v in y]
        gate = [0.5 + 0.5 * jnp.tanh(gv[l, 0, c] * v.astype(F32) + gv[l, 1, c]) for c, v in zip(ids, u)]
        y = [(dot(v, h[1], NT) * q).astype(BF16) for v, q in zip(y, gate)]
        y = [dot(v, f[2], NT).astype(BF16) for v in y]
        y = [(dot(h[2], v, NN) * kt[l, 1]).astype(BF16) for v in y]
        y = [dot(f[3], v, NN).astype(BF16) for v in y]
        for c, v, base in zip(ids, y, u):
            store(c, base.astype(F32) + dot(v, h[3], NT))

    for d in range(1, half):
        ks_copy(d, lax.rem(s + n - 2 * d, n)).wait_recv()
        kf_copy(d, lax.rem(s + n - 2 * d, n)).start()
    for d in range(half):
        kf_copy(d, lax.rem(sib + n - 2 * d, n)).wait_recv()
    lax.fori_loop(0, layers, prepare, 0)

    def step(l, g):
        @pl.when(l == 0)
        def _():
            def arrive(d, _):
                in_wait(g, d)
                return 0

            lax.fori_loop(1, n, arrive, 0)

        compute(l, g)

        @pl.when(l == layers - 1)
        def _():
            def leave(d, _):
                out_copy(g, d).start()
                return 0

            lax.fori_loop(1, n, leave, 0)
            here = pl.ds(g * group, group)
            pltpu.make_async_copy(x.at[here, s], out.at[s, here], out_own.at[g]).start()

    per = maps // groups if maps % groups == 0 else maps
    whole = layers - 2 if layers > 2 else layers

    def layer(l, _):
        sib_arrive(l)

        def one(g, _):
            step(l, g)

            @pl.when(jnp.logical_and(l + 1 < nz - 1, g * per < maps))
            def _():
                for j in range(per):
                    stage(l + 1, g * per + j)

            return 0

        lax.fori_loop(0, groups, one, 0)

        @pl.when(l + 1 < nz - 1)
        def _():
            stage_end(l + 1)

        return 0

    lax.fori_loop(0, whole, layer, 0)

    def last(g, _):
        def one(l, _):
            @pl.when(g == 0)
            def _():
                sib_arrive(l)

            step(l, g)
            return 0

        return lax.fori_loop(whole, layers, one, 0)

    lax.fori_loop(0, groups, last, 0)

    def drain_group(g, _):
        def one(d, _):
            in_copy(g, d).wait_send()
            out_copy(g, d).wait_send()
            out_wait(g, d)
            return 0

        lax.fori_loop(1, n, one, 0)
        here = pl.ds(g * group, group)
        pltpu.make_async_copy(x.at[here, s], out.at[s, here], out_own.at[g]).wait()
        return 0

    lax.fori_loop(0, groups, drain_group, 0)

    for d in range(1, nz):
        for c in kz_copy(d, z):
            c.wait_send()
    for d in range(1, half):
        ks_copy(d, s).wait_send()
    for d in range(half):
        kf_copy(d, lax.rem(s + n - 2 * d, n)).wait_send()

    def drain_layer(l, _):
        @pl.when(z != l)
        def _():
            for r in range(maps):
                sib_copy(l, r).wait_send()

        @pl.when(jnp.logical_and(l <= z, z < nz - 1))
        def _():
            for r in range(maps):
                z_copy(l, r, True).wait_send()

        @pl.when(jnp.logical_and(l >= z, z > 0))
        def _():
            for r in range(maps):
                z_copy(l, r, False).wait_send()

        return 0

    lax.fori_loop(0, layers, drain_layer, 0)


def solution(mesh):
    n, nz = mesh.shape["seq"], mesh.shape["segment"]

    def local(sequence, first, second, kernels, scale, bias):
        rows, local_channels, radix = sequence.shape
        channels = local_channels // n
        group = min(4, channels)
        groups = channels // group
        maps = first.shape[1]
        layers = nz
        total = scale.shape[1]
        x_in = sequence.transpose(1, 0, 2).reshape(n, channels, rows, radix)
        gate = jnp.stack([scale, bias], axis=1)
        sem = pltpu.SemaphoreType.DMA
        anywhere = pl.BlockSpec(memory_space=pl.ANY)
        result = pl.pallas_call(
            functools.partial(kernel, n, nz, group),
            out_shape=jax.ShapeDtypeStruct((n, channels, rows, radix), BF16),
            in_specs=[anywhere] * 5,
            out_specs=anywhere,
            scratch_shapes=[
                pltpu.VMEM((channels, n, rows, radix), BF16),
                pltpu.VMEM((2, layers, maps, radix, radix), BF16),
                pltpu.VMEM((n, layers, 2, rows, radix), BF16),
                pltpu.VMEM((layers, 2, total), F32),
                pltpu.VMEM((layers, 2, radix, radix), F32),
                pltpu.VMEM((layers, 2, channels, 1, radix), F32),
                sem((5,)),
                sem((groups, n)),
                sem((groups, n)),
                sem((groups, n)),
                sem((groups, n)),
                sem((groups,)),
                sem((layers, maps)),
                sem((layers, maps)),
                sem((layers, maps)),
                sem((layers, maps)),
                sem((layers, maps)),
                sem((nz,)),
                sem((nz,)),
                sem((nz,)),
                sem((nz,)),
                sem((n // 2,)),
                sem((n // 2,)),
                sem((n // 2,)),
                sem((n // 2,)),
            ],
            compiler_params=pltpu.CompilerParams(
                collective_id=0, has_side_effects=True, vmem_limit_bytes=56 * 2**20
            ),
        )(x_in, first, second, kernels, gate)
        return result.reshape(local_channels, rows, radix).transpose(1, 0, 2)

    placed = (
        P("seq", "segment", None),
        P("segment", None, None, None),
        P("segment", None, None, None),
        P("segment", None, "seq", None),
        P("segment", None),
        P("segment", None),
    )
    return jax.shard_map(
        local, mesh=mesh, in_specs=placed, out_specs=P("seq", "segment", None), check_vma=False
    )
```

time: 117 us -> 93.1 us (0.80)
  Pallas kernels: 107 us -> 83.4 us
    pallas_call x1, Pallas kernels: 107 us -> 83.4 us  [local(): pl.pallas_call(functools.partial(kernel, n, nz, group), out_shape=jax.Sha...]
where the time goes in v3:
time: 93.1 us; the launch traced here: 92.9 us
  Pallas kernels  83.4 us (90%)
  local copies, waits for them, and re-layouts  8.17 us (9%)
  other arithmetic  1.3 us (1%)
    pallas_call x1, Pallas kernels, local(): pl.pallas_call(functools.partial(kernel, n, nz, group), out_shape=jax.Sha...  83.4 us
    reshape x1, local copies, waits for them, and re-layouts, local(): return result.reshape(local_channels, rows, radix).transpose(1, 0, 2)  4.08 us
    transpose x1, local copies, waits for them, and re-layouts, local(): x_in = sequence.transpose(1, 0, 2).reshape(n, channels, rows, radix)  4.08 us

profile of v3, /device:TPU:25, one launch (start us, length us, event | category | flops | bytes accessed | tf_op | source)
XLA Modules:
  0.0 92.9 jit_solution(10538897647349753035)
XLA Ops:
  0.0 1.3 %pad_maximum_fusion.gate_own = f32[1,2,512]{2,1,0:T(2,128)} fusion(f32[1,1,512]{2,1,0:T(1,128)} %bitcast.11, f32[1,1,512]{2,1,0:T(1,128)} %bitcast.12), kind=kLoop, calls=%fused_computation.1 | loop fusion | flops 1024 | bytes 8192 | tf_op jit(solution)/shard_map/stack | solution.py:358
  1.3 4.1 %copy.7 = bf16[128,32,256]{2,1,0:T(8,128)(2,1)} copy(bf16[128,32,256]{2,0,1:T(8,128)(2,1)} %bitcast.10) | data formatting | bytes 4194304 | tf_op jit(solution)/shard_map/transpose | solution.py:357
  5.4 83.4 %shard_map.64 = bf16[8,16,32,256]{3,2,1,0:T(8,128)(2,1)} custom-call(bf16[8,16,32,256]{3,2,1,0:T(8,128)(2,1)} %bitcast.9, bf16[1,4,256,256]{3,2,1,0:T(8,128)(2,1)} %f_own.1, bf16[1,4,256,256]{3,2,1,0:T(8,128)(2,1)} %g_own.1, bf16[1,2,32,256]{3,2,1,0:T(8,128)(2,1)} %k_own.1, f32[1,2,512]{2,1,0:T(2,128)} %pad_maximum_fusion.gate_own), custom_call_target="tpu_custom_call" | custom-call | tf_op jit(solution)/shard_map/pallas_call | solution.py:361
  88.8 4.1 %copy.10 = bf16[128,32,256]{2,0,1:T(8,128)(2,1)} copy(bf16[128,32,256]{2,1,0:T(8,128)(2,1)} %bitcast.8) | data formatting | bytes 4194304 | tf_op jit(solution)/shard_map/reshape | solution.py:397

commit v4 on v3

--- a/solution.py
+++ b/solution.py
@@ -17,11 +17,11 @@
 
 
 def kernel(
-    n, nz, group, x_in, f_own, g_own, k_own, gate_own, out,
-    x, w, kk, gates, kt, gv,
+    n, nz, group, x_in, f_own, g_own, k_own, scale_own, bias_own, out,
+    x, w, kk, scales, biases, kt, gv,
     own_sem, in_send, in_recv, out_send, out_recv, out_own,
     up_send, down_send, z_recv, sib_send, sib_recv,
-    kz_send, kz_recv, gz_send, gz_recv, ks_send, ks_recv, kf_send, kf_recv,
+    kz_send, kz_recv, gz_send, gz_recv, bz_send, bz_recv, ks_send, ks_recv, kf_send, kf_recv,
 ):
     s, z = lax.axis_index("seq"), lax.axis_index("segment")
     core = lax.rem(s, 2)
@@ -72,7 +72,8 @@
         to = lax.rem(z + d, nz)
         return (
             remote(kk.at[s, l], kk.at[s, l], kz_send.at[d], kz_recv.at[d], segment=to),
-            remote(gates.at[l], gates.at[l], gz_send.at[d], gz_recv.at[d], segment=to),
+            remote(scales.at[l], scales.at[l], gz_send.at[d], gz_recv.at[d], segment=to),
+            remote(biases.at[l], biases.at[l], bz_send.at[d], bz_recv.at[d], segment=to),
         )
 
     def ks_copy(d, owner):
@@ -97,8 +98,9 @@
         pltpu.make_async_copy(f_own.at[0], w.at[0, z], own_sem.at[0]),
         pltpu.make_async_copy(g_own.at[0], w.at[1, z], own_sem.at[1]),
         pltpu.make_async_copy(k_own.at[0], kk.at[s, z], own_sem.at[2]),
-        pltpu.make_async_copy(gate_own.at[0], gates.at[z], own_sem.at[3]),
-        pltpu.make_async_copy(x_in.at[s], x.at[:, s], own_sem.at[4]),
+        pltpu.make_async_copy(scale_own, scales.at[z], own_sem.at[3]),
+        pltpu.make_async_copy(bias_own, biases.at[z], own_sem.at[4]),
+        pltpu.make_async_copy(x_in.at[s], x.at[:, s], own_sem.at[5]),
     ]
     for c in own:
         c.start()
@@ -120,7 +122,7 @@
     lax.fori_loop(1, nz, greet_z, 0)
     pl.semaphore_wait(barrier, n + nz - 2)
 
-    for c in own[:4]:
+    for c in own[:5]:
         c.wait()
 
     for d in range(1, nz):
@@ -140,7 +142,7 @@
         for i in range(maps):
             z_copy(z, i, up).start()
 
-    @pl.when(z == 0)
+    @pl.when(jnp.logical_and(z != 1, z < nz - 1))
     def _():
         send_own(True)
 
@@ -155,7 +157,7 @@
         ks_copy(d, s).start()
     kf_copy(0, s).start()
     lax.fori_loop(1, groups, send_in, 0)
-    own[4].wait()
+    own[5].wait()
 
     def relay(l, i, up):
         c = z_copy(l, i, up)
@@ -176,11 +178,6 @@
         def _():
             relay(z + k + 1, i, False)
 
-    def stage_end(k):
-        @pl.when(jnp.logical_and(z == k + 1, z < nz - 1))
-        def _():
-            send_own(True)
-
     def sib_arrive(l):
         @pl.when(z != l)
         def _():
@@ -189,7 +186,10 @@
 
     for i in range(maps):
         stage(0, i)
-    stage_end(0)
+
+    @pl.when(jnp.logical_and(z == 1, z < nz - 1))
+    def _():
+        send_own(True)
 
     def load(c):
         v = x[c]
@@ -200,7 +200,7 @@
     def store(c, v):
         x[c] = v.reshape(n, rows, radix).astype(BF16)
 
-    total = gates.shape[2]
+    total = scales.shape[2]
     first_channel = (z * n + s) * channels
 
     def prepare(l, _):
@@ -210,9 +210,8 @@
         pick = lax.broadcasted_iota(jnp.int32, (channels, total), 1) == (
             lax.broadcasted_iota(jnp.int32, (channels, total), 0) + first_channel
         )
-        both = gates[l]
-        for i in range(2):
-            col = jnp.sum(jnp.where(pick, both[i : i + 1], 0.0), axis=1, keepdims=True)
+        for i, values in enumerate((scales[l], biases[l])):
+            col = jnp.sum(jnp.where(pick, values, 0.0), axis=1, keepdims=True)
             wide = jnp.broadcast_to(0.5 * col, (channels, radix))
             gv[l, i] = wide.reshape(channels, 1, radix)
         return 0
@@ -262,7 +261,7 @@
             pltpu.make_async_copy(x.at[here, s], out.at[s, here], out_own.at[g]).start()
 
     per = maps // groups if maps % groups == 0 else maps
-    whole = layers - 2 if layers > 2 else layers
+    whole = max(layers - 3, 1)
 
     def layer(l, _):
         sib_arrive(l)
@@ -279,16 +278,17 @@
 
         lax.fori_loop(0, groups, one, 0)
 
-        @pl.when(l + 1 < nz - 1)
-        def _():
-            stage_end(l + 1)
-
         return 0
 
     lax.fori_loop(0, whole, layer, 0)
 
     def last(g, _):
         def one(l, _):
+            @pl.when(jnp.logical_and(g == 0, jnp.logical_and(l > whole, l < nz - 1)))
+            def _():
+                for i in range(maps):
+                    stage(l, i)
+
             @pl.when(g == 0)
             def _():
                 sib_arrive(l)
@@ -355,22 +355,22 @@
         layers = nz
         total = scale.shape[1]
         x_in = sequence.transpose(1, 0, 2).reshape(n, channels, rows, radix)
-        gate = jnp.stack([scale, bias], axis=1)
         sem = pltpu.SemaphoreType.DMA
         anywhere = pl.BlockSpec(memory_space=pl.ANY)
         result = pl.pallas_call(
             functools.partial(kernel, n, nz, group),
             out_shape=jax.ShapeDtypeStruct((n, channels, rows, radix), BF16),
-            in_specs=[anywhere] * 5,
+            in_specs=[anywhere] * 6,
             out_specs=anywhere,
             scratch_shapes=[
                 pltpu.VMEM((channels, n, rows, radix), BF16),
                 pltpu.VMEM((2, layers, maps, radix, radix), BF16),
                 pltpu.VMEM((n, layers, 2, rows, radix), BF16),
-                pltpu.VMEM((layers, 2, total), F32),
+                pltpu.VMEM((layers, 1, total), F32),
+                pltpu.VMEM((layers, 1, total), F32),
                 pltpu.VMEM((layers, 2, radix, radix), F32),
                 pltpu.VMEM((layers, 2, channels, 1, radix), F32),
-                sem((5,)),
+                sem((6,)),
                 sem((groups, n)),
                 sem((groups, n)),
                 sem((groups, n)),
@@ -385,6 +385,8 @@
                 sem((nz,)),
                 sem((nz,)),
                 sem((nz,)),
+                sem((nz,)),
+                sem((nz,)),
                 sem((n // 2,)),
                 sem((n // 2,)),
                 sem((n // 2,)),
@@ -393,7 +395,7 @@
             compiler_params=pltpu.CompilerParams(
                 collective_id=0, has_side_effects=True, vmem_limit_bytes=56 * 2**20
             ),
-        )(x_in, first, second, kernels, gate)
+        )(x_in, first, second, kernels, scale, bias)
         return result.reshape(local_channels, rows, radix).transpose(1, 0, 2)
 
     placed = (

time: 93.1 us -> 83.8 us (0.900)
  Pallas kernels: 83.4 us -> 75.5 us
  other arithmetic: 1.3 us -> 0 us
    pallas_call x1, Pallas kernels: 83.4 us -> 75.5 us  [local(): pl.pallas_call(functools.partial(kernel, n, nz, group), out_shape=jax.Sha...]
    another operation x1 -> x0, other arithmetic: 1.3 us -> none  [local(): gate = jnp.stack([scale, bias], axis=1)]
where the time goes in v4:
time: 83.8 us; the launch traced here: 83.7 us
  Pallas kernels  75.5 us (90%)
  local copies, waits for them, and re-layouts  8.17 us (10%)
    pallas_call x1, Pallas kernels, local(): pl.pallas_call(functools.partial(kernel, n, nz, group), out_shape=jax.Sha...  75.5 us
    reshape x1, local copies, waits for them, and re-layouts, local(): return result.reshape(local_channels, rows, radix).transpose(1, 0, 2)  4.08 us
    transpose x1, local copies, waits for them, and re-layouts, local(): x_in = sequence.transpose(1, 0, 2).reshape(n, channels, rows, radix)  4.08 us

profile of v4, /device:TPU:25, one launch (start us, length us, event | category | flops | bytes accessed | tf_op | source)
XLA Modules:
  0.0 83.7 jit_solution(4125629216800715212)
XLA Ops:
  0.0 4.1 %copy.7 = bf16[128,32,256]{2,1,0:T(8,128)(2,1)} copy(bf16[128,32,256]{2,0,1:T(8,128)(2,1)} %bitcast.8) | data formatting | bytes 4194304 | tf_op jit(solution)/shard_map/transpose | solution.py:357
  4.1 75.5 %shard_map.64 = bf16[8,16,32,256]{3,2,1,0:T(8,128)(2,1)} custom-call(bf16[8,16,32,256]{3,2,1,0:T(8,128)(2,1)} %bitcast.7, bf16[1,4,256,256]{3,2,1,0:T(8,128)(2,1)} %f_own.1, bf16[1,4,256,256]{3,2,1,0:T(8,128)(2,1)} %g_own.1, bf16[1,2,32,256]{3,2,1,0:T(8,128)(2,1)} %k_own.1, f32[1,512]{1,0:T(1,128)} %scale_own.1, f32[1,512]{1,0:T(1,128)} %bias_own.1), custom_call_target="tpu_custom_call" | custom-call | tf_op jit(solution)/shard_map/pallas_call | solution.py:360
  79.6 4.1 %copy.10 = bf16[128,32,256]{2,0,1:T(8,128)(2,1)} copy(bf16[128,32,256]{2,1,0:T(8,128)(2,1)} %bitcast.6) | data formatting | bytes 4194304 | tf_op jit(solution)/shard_map/reshape | solution.py:399

commit v5 on v4

--- a/solution.py
+++ b/solution.py
@@ -17,9 +17,9 @@
 
 
 def kernel(
-    n, nz, group, x_in, f_own, g_own, k_own, scale_own, bias_own, out,
-    x, w, kk, scales, biases, kt, gv,
-    own_sem, in_send, in_recv, out_send, out_recv, out_own,
+    n, nz, group, seq_in, f_own, g_own, k_own, scale_own, bias_own, out,
+    raw, x_in, x, w, kk, scales, biases, kt, gv,
+    own_sem, raw_sem, in_send, in_recv, out_send, out_recv, out_own,
     up_send, down_send, z_recv, sib_send, sib_recv,
     kz_send, kz_recv, gz_send, gz_recv, bz_send, bz_recv, ks_send, ks_recv, kf_send, kf_recv,
 ):
@@ -100,10 +100,15 @@
         pltpu.make_async_copy(k_own.at[0], kk.at[s, z], own_sem.at[2]),
         pltpu.make_async_copy(scale_own, scales.at[z], own_sem.at[3]),
         pltpu.make_async_copy(bias_own, biases.at[z], own_sem.at[4]),
-        pltpu.make_async_copy(x_in.at[s], x.at[:, s], own_sem.at[5]),
     ]
+    def raw_copy(d):
+        t = peer(d)
+        return pltpu.make_async_copy(seq_in.at[:, t], raw.at[t], raw_sem.at[d])
+
     for c in own:
         c.start()
+    for d in range(1, n + 1):
+        raw_copy(d % n).start()
 
     barrier = pltpu.get_barrier_semaphore()
     mesh_id = pl.DeviceIdType.MESH
@@ -122,7 +127,7 @@
     lax.fori_loop(1, nz, greet_z, 0)
     pl.semaphore_wait(barrier, n + nz - 2)
 
-    for c in own[:5]:
+    for c in own:
         c.wait()
 
     for d in range(1, nz):
@@ -136,7 +141,19 @@
 
         return lax.fori_loop(1, n, one, 0)
 
-    send_in(0, 0)
+    def turned(d):
+        raw_copy(d).wait()
+        v = raw[peer(d)]
+        return jnp.swapaxes(v, 0, 1)
+
+    def turn(d, _):
+        x_in[peer(d)] = turned(d)
+
+        @pl.when(d > 1)
+        def _():
+            in_copy(0, d - 1).start()
+
+        return 0
 
     def send_own(up):
         for i in range(maps):
@@ -149,6 +166,10 @@
     @pl.when(z > 0)
     def _():
         send_own(False)
+
+    lax.fori_loop(1, n, turn, 0)
+    x[:, pl.ds(s, 1)] = turned(0)[:, None]
+    in_copy(0, n - 1).start()
 
     for d in range(1, nz):
         for c in kz_copy(d, lax.rem(z + nz - d, nz)):
@@ -157,7 +178,6 @@
         ks_copy(d, s).start()
     kf_copy(0, s).start()
     lax.fori_loop(1, groups, send_in, 0)
-    own[5].wait()
 
     def relay(l, i, up):
         c = z_copy(l, i, up)
@@ -354,7 +374,7 @@
         maps = first.shape[1]
         layers = nz
         total = scale.shape[1]
-        x_in = sequence.transpose(1, 0, 2).reshape(n, channels, rows, radix)
+        x_in = sequence.reshape(rows, n, channels, radix)
         sem = pltpu.SemaphoreType.DMA
         anywhere = pl.BlockSpec(memory_space=pl.ANY)
         result = pl.pallas_call(
@@ -363,6 +383,8 @@
             in_specs=[anywhere] * 6,
             out_specs=anywhere,
             scratch_shapes=[
+                pltpu.VMEM((n, rows, channels, radix), BF16),
+                pltpu.VMEM((n, channels, rows, radix), BF16),
                 pltpu.VMEM((channels, n, rows, radix), BF16),
                 pltpu.VMEM((2, layers, maps, radix, radix), BF16),
                 pltpu.VMEM((n, layers, 2, rows, radix), BF16),
@@ -370,7 +392,8 @@
                 pltpu.VMEM((layers, 1, total), F32),
                 pltpu.VMEM((layers, 2, radix, radix), F32),
                 pltpu.VMEM((layers, 2, channels, 1, radix), F32),
-                sem((6,)),
+                sem((5,)),
+                sem((n,)),
                 sem((groups, n)),
                 sem((groups, n)),
                 sem((groups, n)),

time: 83.8 us -> 79.9 us (0.953)
  local copies, waits for them, and re-layouts: 8.17 us -> 4.08 us
    transpose x1 -> x0, local copies, waits for them, and re-layouts: 4.08 us -> none  [local(): x_in = sequence.transpose(1, 0, 2).reshape(n, channels, rows, radix)]
where the time goes in v5:
time: 79.9 us; the launch traced here: 79.8 us
  Pallas kernels  75.7 us (95%)
  local copies, waits for them, and re-layouts  4.08 us (5%)
    pallas_call x1, Pallas kernels, local(): pl.pallas_call(functools.partial(kernel, n, nz, group), out_shape=jax.Sha...  75.7 us
    reshape x1, local copies, waits for them, and re-layouts, local(): return result.reshape(local_channels, rows, radix).transpose(1, 0, 2)  4.08 us

profile of v5, /device:TPU:25, one launch (start us, length us, event | category | flops | bytes accessed | tf_op | source)
XLA Modules:
  0.0 79.8 jit_solution(8648447642543592159)
XLA Ops:
  0.0 75.7 %shard_map.64 = bf16[8,16,32,256]{3,2,1,0:T(8,128)(2,1)} custom-call(bf16[32,8,16,256]{3,2,1,0:T(8,128)(2,1)} %bitcast.6, bf16[1,4,256,256]{3,2,1,0:T(8,128)(2,1)} %f_own.1, bf16[1,4,256,256]{3,2,1,0:T(8,128)(2,1)} %g_own.1, bf16[1,2,32,256]{3,2,1,0:T(8,128)(2,1)} %k_own.1, f32[1,512]{1,0:T(1,128)} %scale_own.1, f32[1,512]{1,0:T(1,128)} %bias_own.1), custom_call_target="tpu_custom_call" | custom-call | tf_op jit(solution)/shard_map/pallas_call | solution.py:380
  75.7 4.1 %copy.9 = bf16[128,32,256]{2,0,1:T(8,128)(2,1)} copy(bf16[128,32,256]{2,1,0:T(8,128)(2,1)} %bitcast.5) | data formatting | bytes 4194304 | tf_op jit(solution)/shard_map/reshape | solution.py:422

commit v6 on v5

--- a/solution.py
+++ b/solution.py
@@ -189,14 +189,19 @@
 
         sib_copy(l, i).start()
 
+    def rise(k, i):
+        @pl.when(z > k)
+        def _():
+            relay(k, i, True)
+
+    def fall(k, i):
+        @pl.when(z + k + 1 < nz)
+        def _():
+            relay(z + k + 1, i, False)
+
     def stage(k, i):
-        @pl.when(z > k)
-        def _():
-            relay(k, i, True)
-
-        @pl.when(z + k + 1 < nz)
-        def _():
-            relay(z + k + 1, i, False)
+        rise(k, i)
+        fall(k, i)
 
     def sib_arrive(l):
         @pl.when(z != l)
@@ -283,13 +288,24 @@
     per = maps // groups if maps % groups == 0 else maps
     whole = max(layers - 3, 1)
 
+    passes_on = jnp.logical_and(z > 0, z < nz - 1)
+
     def layer(l, _):
+        @pl.when(jnp.logical_and(l + 1 < nz - 1, passes_on))
+        def _():
+            for i in range(maps):
+                stage(l + 1, i)
+
         sib_arrive(l)
 
         def one(g, _):
             step(l, g)
 
-            @pl.when(jnp.logical_and(l + 1 < nz - 1, g * per < maps))
+            @pl.when(
+                jnp.logical_and(
+                    jnp.logical_and(l + 1 < nz - 1, g * per < maps), jnp.logical_not(passes_on)
+                )
+            )
             def _():
                 for j in range(per):
                     stage(l + 1, g * per + j)
@@ -307,7 +323,12 @@
             @pl.when(jnp.logical_and(g == 0, jnp.logical_and(l > whole, l < nz - 1)))
             def _():
                 for i in range(maps):
-                    stage(l, i)
+                    rise(l, i)
+
+            @pl.when(jnp.logical_and(g == 0, jnp.logical_and(l > whole + 1, l < nz)))
+            def _():
+                for i in range(maps):
+                    fall(l - 1, i)
 
             @pl.when(g == 0)
             def _():

time: 79.9 us -> 78.5 us (0.982)
  Pallas kernels: 75.7 us -> 74.3 us
    pallas_call x1, Pallas kernels: 75.7 us -> 74.3 us  [local(): pl.pallas_call(functools.partial(kernel, n, nz, group), out_shape=jax.Sha...]
where the time goes in v6:
time: 78.5 us; the launch traced here: 78.4 us
  Pallas kernels  74.3 us (95%)
  local copies, waits for them, and re-layouts  4.08 us (5%)
    pallas_call x1, Pallas kernels, local(): pl.pallas_call(functools.partial(kernel, n, nz, group), out_shape=jax.Sha...  74.3 us
    reshape x1, local copies, waits for them, and re-layouts, local(): return result.reshape(local_channels, rows, radix).transpose(1, 0, 2)  4.08 us

profile of v6, /device:TPU:25, one launch (start us, length us, event | category | flops | bytes accessed | tf_op | source)
XLA Modules:
  0.0 78.4 jit_solution(4725350328320752532)
XLA Ops:
  0.0 74.3 %shard_map.64 = bf16[8,16,32,256]{3,2,1,0:T(8,128)(2,1)} custom-call(bf16[32,8,16,256]{3,2,1,0:T(8,128)(2,1)} %bitcast.6, bf16[1,4,256,256]{3,2,1,0:T(8,128)(2,1)} %f_own.1, bf16[1,4,256,256]{3,2,1,0:T(8,128)(2,1)} %g_own.1, bf16[1,2,32,256]{3,2,1,0:T(8,128)(2,1)} %k_own.1, f32[1,512]{1,0:T(1,128)} %scale_own.1, f32[1,512]{1,0:T(1,128)} %bias_own.1), custom_call_target="tpu_custom_call" | custom-call | tf_op jit(solution)/shard_map/pallas_call | solution.py:401
  74.3 4.1 %copy.9 = bf16[128,32,256]{2,0,1:T(8,128)(2,1)} copy(bf16[128,32,256]{2,1,0:T(8,128)(2,1)} %bitcast.5) | data formatting | bytes 4194304 | tf_op jit(solution)/shard_map/reshape | solution.py:443
